TPU v7x, 256 devices: a whole 4x4x8 slice. The times are simulated.
256 devices in a mesh: grp: 4 (over z_lo), row: 4 (over x), col: 16 (over y, z_hi, core).
Axes of the slice: x: 4, y: 4, z: 8 (z_hi: 2, z_lo: 4; z = z_hi * 4 + z_lo), core: 2. Of those that a mesh axis runs over, the one named last changes fastest.
Arguments:
- outer_params: float32 [8192, 1024], P('col', 'row'), may hold values from -0.0625 to 0.0625
- first_moment: float32 [4, 8192, 1024], P('grp', 'col', 'row'), may hold values from -0.12 to 0.12
- second_moment: float32 [4, 8192, 1024], P('grp', 'col', 'row'), may hold values from 0.0001 to 0.01
- outer_moment: float32 [8192, 1024], P('col', 'row'), may hold values from -0.06 to 0.06
- activations: bfloat16 [4, 3, 2048, 8192], P('grp', None, 'row', 'col'), may hold values from -6 to 6
- targets: bfloat16 [4, 3, 2048, 1024], P('grp', None, 'col', 'row'), may hold values from -6 to 6
Outputs:
- new_params: float32 [8192, 1024], P('col', 'row')
- new_moment: float32 [8192, 1024], P('col', 'row')
All inputs are finite; a program needn't handle non-finite values.
Results may differ from a plain program's by a relative error of at most 0.0054.
Values may be sent and summed in bfloat16 or wider, within the bound.
A program may use at most 64 MiB of HBM per device.

v0:
```python
import jax
import jax.numpy as jnp
from jax import lax
from jax.sharding import Mesh
from jax.sharding import PartitionSpec as P

TOKENS = 2048
STEPS = 3
SLOW_STEPS = 1
PRIOR = 100
COL = ("col_0", "col_1", "col_2")


beta_first = 0.9
beta_second = 0.95
inner_rate = 0.01
decay_rate = 0.1
epsilon_value = 1e-08
outer_rate = 0.7
momentum_coef = 0.9


def split_up(shard, dim, count):
    before, after = (shard.shape[:dim], shard.shape[dim + 1 :])
    return jnp.moveaxis(shard.reshape(*before, count, -1, *after), dim, 0)


def summed_on_arrival(shard, axis, dim):
    count = lax.axis_size(axis)
    parts = lax.all_to_all(split_up(shard, dim, count), axis, 0, 0, tiled=True)
    return jnp.sum(parts, axis=0)


def sum_in_two_steps(shard, axes, dim):
    far, near = axes
    own = summed_on_arrival(split_up(shard, dim, lax.axis_size(far)), near, dim + 1)
    return jnp.sum(lax.all_to_all(own, far, 0, 0, tiled=True), axis=0)


def filled_up(lines, count):
    spare = -lines.shape[0] % count
    if not spare:
        return lines
    return jnp.concatenate([lines, jnp.zeros((spare, *lines.shape[1:]), lines.dtype)])


def sent_to_all(shard, axis):
    copies = jnp.broadcast_to(shard, (lax.axis_size(axis), *shard.shape))
    return lax.all_to_all(copies, axis, split_axis=0, concat_axis=0, tiled=True)


def in_order(parts, dim):
    shape = list(parts.shape[1:])
    shape[dim] *= parts.shape[0]
    return jnp.moveaxis(parts, 0, dim).reshape(shape)


def whole_of(shard, axes, dim):
    far, near = axes
    parts = sent_to_all(sent_to_all(shard, far), near)
    return in_order(parts.swapaxes(0, 1).reshape(-1, *shard.shape), dim)


def total_of(shard, axes):
    lines = shard.reshape(-1, shard.shape[-1])
    own = sum_in_two_steps(
        filled_up(lines, lax.axis_size(axes[0]) * lax.axis_size(axes[1])), axes, 0
    )
    whole = whole_of(own, axes, 0)
    return whole[: len(lines)].reshape(shard.shape)


def over_copies(shard, axis):
    everything = sent_to_all(shard, axis)
    return jnp.sum(everything, axis=0)


def local(outer_params, first_moment, second_moment, outer_moment, activations, targets):
    unit = lax.axis_index("grp")
    gathered = lax.all_gather(activations[0], "row", axis=1, tiled=True)
    wanted_all = targets[0]
    wanted_all = lax.all_gather(wanted_all, COL, axis=1, tiled=True)
    first = first_moment[0]
    second = second_moment[0]
    params = outer_params
    for inner_step in range(STEPS):
        inputs = gathered[inner_step]
        partial_value = jnp.dot(
            inputs, params.astype(jnp.bfloat16), preferred_element_type=jnp.float32
        )
        output = total_of(partial_value, (("col_0", "col_1"), "col_2"))
        residual = (output - wanted_all[inner_step].astype(jnp.float32)).astype(jnp.bfloat16)
        gradient = (
            lax.dot_general(
                inputs, residual, (((0,), (0,)), ((), ())), preferred_element_type=jnp.float32
            )
            / TOKENS
        )
        first_next = beta_first * first + (1.0 - beta_first) * gradient
        second_next = beta_second * second + (1.0 - beta_second) * gradient * gradient
        power = PRIOR + inner_step + 1
        corrected = (
            first_next
            / (1.0 - beta_first**power)
            / (jnp.sqrt(second_next / (1.0 - beta_second**power)) + epsilon_value)
        )
        params_next = params - inner_rate * (corrected + decay_rate * params)
        active = jnp.logical_or(unit < 3, inner_step < SLOW_STEPS)
        params = jnp.where(active, params_next, params)
        first = jnp.where(active, first_next, first)
        second = jnp.where(active, second_next, second)
    total_steps = float(3 * STEPS + SLOW_STEPS)
    weight = jnp.where(unit < 3, float(STEPS), float(SLOW_STEPS)) / total_steps
    term = weight * (outer_params - params)
    pseudo = over_copies(term, "grp")
    new_moment = momentum_coef * outer_moment + pseudo
    new_params = outer_params - outer_rate * (pseudo + momentum_coef * new_moment)
    return (new_params, new_moment)


def solution(mesh):
    finer = Mesh(
        mesh.devices.reshape(mesh.shape["grp"], mesh.shape["row"], 4, 2, 2),
        ("grp", "row", "col_0", "col_1", "col_2"),
    )
    placed = (
        P(COL, "row"),
        P("grp", COL, "row"),
        P("grp", COL, "row"),
        P(COL, "row"),
        P("grp", None, "row", COL),
        P("grp", None, COL, "row"),
    )
    return jax.shard_map(
        local,
        mesh=finer,
        in_specs=placed,
        out_specs=(P(COL, "row"), P(COL, "row")),
        check_vma=False,
    )
```

profile of v0, /device:TPU:1, one launch (start us, length us, event | category | flops | bytes accessed | tf_op | source)
XLA Modules:
  0.0 409.2 jit_solution(15068283860982565642)
XLA Ops:
  8.7 73.2 %all-gather.5.cloned.1.call-done = bf16[1,3,2048,512]{3,2,1,0:T(8,128)(2,1)} async-done(((bf16[1,3,512,512]{3,2,1,0:T(8,128)(2,1)}), bf16[1,3,2048,512]{3,2,1,0:T(8,128)(2,1)}) %all-gather.5.cloned.1.call-update) | async-done | bytes 6291472 | tf_op jit(solution)/shard_map/all_gather | solution.py:80
  81.8 1.6 slice-done.6
  84.3 5.8 %all_to_all.65 = f32[2,8,128,256]{3,2,1,0:T(8,128)S(1)} all-to-all(f32[2,8,128,256]{3,2,1,0:T(8,128)S(1)} %copy.76), channel_id=1, replica_groups=mesh['grp'=4,'row'=4,'col_0'=4,'col_1'=2,'col_2'=2] {'col_2'}, dimensions={0} | all-to-all | bytes 4194304 | tf_op jit(solution)/shard_map/all_to_all | solution.py:30
  90.3 35.3 %all_to_all.66 = f32[8,128,256]{2,1,0:T(8,128)S(1)} all-to-all(f32[8,128,256]{2,1,0:T(8,128)S(1)} %reduce_sum.63), channel_id=1, replica_groups=mesh['grp'=4,'row'=4,'col_0'=4,'col_1'=2,'col_2'=2] {'col_0','col_1'}, dimensions={0} | all-to-all | bytes 2097152 | tf_op jit(solution)/shard_map/all_to_all | solution.py:37
  125.7 1.1 broadcast_in_dim.21
  126.8 7.7 %all-to-all-start.2 = ((f32[8,128,256]{2,1,0:T(8,128)}), f32[8,128,256]{2,1,0:T(8,128)S(1)}, u32[]{:S(2)}, u32[]{:S(2)}) async-start(f32[8,128,256]{2,1,0:T(8,128)} %broadcast_in_dim.21), calls=%async_computation.2 | async-start | bytes 2097152 | tf_op jit(solution)/shard_map/all_to_all | solution.py:49
  134.8 1.0 copy.75
  136.0 35.4 %all-gather.7.cloned.1.call-done = bf16[1,3,2048,256]{3,2,1,0:T(8,128)(2,1)} async-done(((bf16[1,3,128,256]{3,2,1,0:T(8,128)(2,1)}), bf16[1,3,2048,256]{3,2,1,0:T(8,128)(2,1)}) %all-gather.7.cloned.1.call-update) | async-done | bytes 3145744 | tf_op jit(solution)/shard_map/all_gather | solution.py:82
  171.4 3.4 fusion.43
  175.0 5.7 %all_to_all.67 = f32[2,8,128,256]{3,2,1,0:T(8,128)S(1)} all-to-all(f32[2,8,128,256]{3,2,1,0:T(8,128)S(1)} %broadcast_in_dim.22), channel_id=1, replica_groups=mesh['grp'=4,'row'=4,'col_0'=4,'col_1'=2,'col_2'=2] {'col_2'}, dimensions={0} | all-to-all | bytes 4194304 | tf_op jit(solution)/shard_map/all_to_all | solution.py:49
  182.7 2.4 convolution_bitcast_fusion.1
  185.2 3.0 reshape_reshape.4
  188.3 5.4 %all_to_all.68 = f32[2,8,128,256]{2,1,3,0:T(8,128)S(1)} all-to-all(f32[2,8,128,256]{2,1,3,0:T(8,128)S(1)} %bitcast.148), channel_id=1, replica_groups=mesh['grp'=4,'row'=4,'col_0'=4,'col_1'=2,'col_2'=2] {'col_2'}, dimensions={0} | all-to-all | bytes 4194304 | tf_op jit(solution)/shard_map/all_to_all | solution.py:30
  194.2 21.3 %all_to_all.69 = f32[8,128,256]{1,2,0:T(8,128)S(1)} all-to-all(f32[8,128,256]{1,2,0:T(8,128)S(1)} %copy.83), channel_id=1, replica_groups=mesh['grp'=4,'row'=4,'col_0'=4,'col_1'=2,'col_2'=2] {'col_0','col_1'}, dimensions={0} | all-to-all | bytes 2097152 | tf_op jit(solution)/shard_map/all_to_all | solution.py:37
  215.7 1.0 broadcast_in_dim.23
  216.7 3.6 all-to-all-start.6
  220.3 24.7 %all-to-all-done.6 = f32[8,128,256]{2,1,0:T(8,128)S(1)} async-done(((f32[8,128,256]{2,1,0:T(8,128)}), f32[8,128,256]{2,1,0:T(8,128)S(1)}, u32[]{:S(2)}, u32[]{:S(2)}) %all-to-all-start.6) | async-done | bytes 1048608 | tf_op jit(solution)/shard_map/all_to_all | solution.py:49
  245.2 6.0 %all_to_all.70 = f32[2,8,128,256]{3,2,1,0:T(8,128)S(1)} all-to-all(f32[2,8,128,256]{3,2,1,0:T(8,128)S(1)} %broadcast_in_dim.24), channel_id=1, replica_groups=mesh['grp'=4,'row'=4,'col_0'=4,'col_1'=2,'col_2'=2] {'col_2'}, dimensions={0} | all-to-all | bytes 4194304 | tf_op jit(solution)/shard_map/all_to_all | solution.py:49
  253.1 2.9 convolution_bitcast_fusion
  256.0 3.0 reshape_reshape.5
  259.2 5.4 %all_to_all.71 = f32[2,8,128,256]{2,1,3,0:T(8,128)S(1)} all-to-all(f32[2,8,128,256]{2,1,3,0:T(8,128)S(1)} %bitcast.149), channel_id=1, replica_groups=mesh['grp'=4,'row'=4,'col_0'=4,'col_1'=2,'col_2'=2] {'col_2'}, dimensions={0} | all-to-all | bytes 4194304 | tf_op jit(solution)/shard_map/all_to_all | solution.py:30
  265.1 25.3 %all_to_all.72 = f32[8,128,256]{1,2,0:T(8,128)S(1)} all-to-all(f32[8,128,256]{1,2,0:T(8,128)S(1)} %copy.89), channel_id=1, replica_groups=mesh['grp'=4,'row'=4,'col_0'=4,'col_1'=2,'col_2'=2] {'col_0','col_1'}, dimensions={0} | all-to-all | bytes 2097152 | tf_op jit(solution)/shard_map/all_to_all | solution.py:37
  290.5 1.0 broadcast_in_dim.25
  291.5 3.6 all-to-all-start.10
  295.1 20.5 %all-to-all-done.10 = f32[8,128,256]{2,1,0:T(8,128)S(1)} async-done(((f32[8,128,256]{2,1,0:T(8,128)}), f32[8,128,256]{2,1,0:T(8,128)S(1)}, u32[]{:S(2)}, u32[]{:S(2)}) %all-to-all-start.10) | async-done | bytes 1048608 | tf_op jit(solution)/shard_map/all_to_all | solution.py:49
  315.8 6.9 %all_to_all.73 = f32[2,8,128,256]{3,2,1,0:T(8,128)S(1)} all-to-all(f32[2,8,128,256]{3,2,1,0:T(8,128)S(1)} %broadcast_in_dim.26), channel_id=1, replica_groups=mesh['grp'=4,'row'=4,'col_0'=4,'col_1'=2,'col_2'=2] {'col_2'}, dimensions={0} | all-to-all | bytes 4194304 | tf_op jit(solution)/shard_map/all_to_all | solution.py:49
  324.4 3.4 fusion.8
  328.0 1.5 broadcast_in_dim.27
  329.5 20.7 %all-to-all-start.12 = ((f32[4,512,256]{2,1,0:T(8,128)}), f32[4,512,256]{2,1,0:T(8,128)S(1)}, u32[]{:S(2)}, u32[]{:S(2)}) async-start(f32[4,512,256]{2,1,0:T(8,128)} %broadcast_in_dim.27), calls=%async_computation.12 | async-start | bytes 4194304 | tf_op jit(solution)/shard_map/all_to_all | solution.py:49
  350.3 1.2 copy.95
  351.5 46.5 %all-to-all-done.12 = f32[4,512,256]{2,1,0:T(8,128)S(1)} async-done(((f32[4,512,256]{2,1,0:T(8,128)}), f32[4,512,256]{2,1,0:T(8,128)S(1)}, u32[]{:S(2)}, u32[]{:S(2)}) %all-to-all-start.12) | async-done | bytes 2097184 | tf_op jit(solution)/shard_map/all_to_all | solution.py:49
  399.0 1.2 copy.97
  (90 shorter events, 13.9 us)
Async XLA Ops:
  7.2 74.7 %all-gather.5.cloned.1.call-start = ((), (), s32[]{:S(2)}) async-start(), calls=%async_computation.13 | async-start | bytes 7864320 | tf_op jit(solution)/shard_map/all_gather | solution.py:80
  7.9 163.5 %all-gather.7.cloned.1.call-start = ((), (), s32[]{:S(2)}) async-start(), calls=%async_computation.14 | async-start | bytes 3342336 | tf_op jit(solution)/shard_map/all_gather | solution.py:82
  8.6 73.2 %copy-start.2 = (f32[512,256]{1,0:T(8,128)S(1)}, f32[512,256]{1,0:T(8,128)}, u32[]{:S(2)}) copy-start(f32[512,256]{1,0:T(8,128)} %param.6) | copy-start | bytes 1572868
  81.8 1.6 slice-start.6
  125.6 8.9 %copy-start.3 = (f32[512,256]{1,0:T(8,128)S(1)}, f32[512,256]{1,0:T(8,128)}, u32[]{:S(2)}) copy-start(f32[512,256]{1,0:T(8,128)} %param.6) | copy-start | bytes 1572868
  125.7 9.1 %copy-start.7 = (f32[1,512,256]{2,1,0:T(8,128)S(1)}, f32[1,512,256]{2,1,0:T(8,128)}, u32[]{:S(2)}) copy-start(f32[1,512,256]{2,1,0:T(8,128)} %param.7) | copy-start | bytes 1572868
  126.8 9.0 %copy-start.8 = (f32[1,512,256]{2,1,0:T(8,128)S(1)}, f32[1,512,256]{2,1,0:T(8,128)}, u32[]{:S(2)}) copy-start(f32[1,512,256]{2,1,0:T(8,128)} %param.8) | copy-start | bytes 1572868
  126.8 47.9 %all-to-all-start.2 = ((f32[8,128,256]{2,1,0:T(8,128)}), f32[8,128,256]{2,1,0:T(8,128)S(1)}, u32[]{:S(2)}, u32[]{:S(2)}) async-start(f32[8,128,256]{2,1,0:T(8,128)} %broadcast_in_dim.21), calls=%async_computation.2 | async-start | bytes 2097152 | tf_op jit(solution)/shard_map/all_to_all | solution.py:49
  134.8 47.1 %copy-start.4 = (f32[512,256]{0,1:T(8,128)}, f32[512,256]{0,1:T(8,128)S(1)}, u32[]{:S(2)}) copy-start(f32[512,256]{0,1:T(8,128)S(1)} %copy.98) | copy-start | bytes 1572868
  136.0 45.9 %copy-start.12 = (f32[1,512,256]{1,2,0:T(8,128)}, f32[1,512,256]{1,2,0:T(8,128)S(1)}, u32[]{:S(2)}) copy-start(f32[1,512,256]{1,2,0:T(8,128)S(1)} %copy.78) | copy-start | bytes 1572868
  174.8 6.3 %slice-start = ((s8[6291456]{0:T(1024)(128)(4,1)}), s8[4194304]{0:T(1024)(128)(4,1)S(1)}, s32[]{:S(2)}) async-start(s8[6291456]{0:T(1024)(128)(4,1)} %bitcast.150), calls=%async_computation.15 | async-start | bytes 8388608
  175.0 6.1 %slice-start.1 = ((s8[6291456]{0:T(1024)(128)(4,1)}), s8[2097152]{0:T(1024)(128)(4,1)S(1)}, s32[]{:S(2)}) async-start(s8[6291456]{0:T(1024)(128)(4,1)} %bitcast.150), calls=%async_computation.16 | async-start | bytes 4194304
  181.1 1.6 copy-start.9
  181.9 0.9 copy-start.15
  216.7 28.3 %all-to-all-start.6 = ((f32[8,128,256]{2,1,0:T(8,128)}), f32[8,128,256]{2,1,0:T(8,128)S(1)}, u32[]{:S(2)}, u32[]{:S(2)}) async-start(f32[8,128,256]{2,1,0:T(8,128)} %broadcast_in_dim.23), calls=%async_computation.6 | async-start | bytes 2097152 | tf_op jit(solution)/shard_map/all_to_all | solution.py:49
  245.0 6.5 %slice-start.2 = ((s8[6291456]{0:T(1024)(128)(4,1)}), s8[4194304]{0:T(1024)(128)(4,1)S(1)}, s32[]{:S(2)}) async-start(s8[6291456]{0:T(1024)(128)(4,1)} %bitcast.152), calls=%async_computation.17 | async-start | bytes 8388608
  245.2 6.0 %copy-start.1 = (bf16[1,1,2048,256]{3,2,1,0:T(8,128)(2,1)S(1)}, bf16[1,1,2048,256]{3,2,1,0:T(8,128)(2,1)}, u32[]{:S(2)}) copy-start(bf16[1,1,2048,256]{3,2,1,0:T(8,128)(2,1)} %get-tuple-element.13) | copy-start | bytes 3145732
  245.2 6.3 %slice-start.3 = ((s8[6291456]{0:T(1024)(128)(4,1)}), s8[2097152]{0:T(1024)(128)(4,1)S(1)}, s32[]{:S(2)}) async-start(s8[6291456]{0:T(1024)(128)(4,1)} %bitcast.152), calls=%async_computation.18 | async-start | bytes 4194304
  251.6 1.6 copy-start.5
  251.6 1.6 copy-start.10
  251.6 1.5 copy-start.13
  251.6 1.5 copy-start.16
  291.5 24.0 %all-to-all-start.10 = ((f32[8,128,256]{2,1,0:T(8,128)}), f32[8,128,256]{2,1,0:T(8,128)S(1)}, u32[]{:S(2)}, u32[]{:S(2)}) async-start(f32[8,128,256]{2,1,0:T(8,128)} %broadcast_in_dim.25), calls=%async_computation.10 | async-start | bytes 2097152 | tf_op jit(solution)/shard_map/all_to_all | solution.py:49
  315.6 7.5 %slice-start.4 = ((s8[6291456]{0:T(1024)(128)(4,1)}), s8[4194304]{0:T(1024)(128)(4,1)S(1)}, s32[]{:S(2)}) async-start(s8[6291456]{0:T(1024)(128)(4,1)} %bitcast.154), calls=%async_computation.19 | async-start | bytes 8388608
  315.8 6.9 %copy-start = (bf16[1,1,2048,256]{3,2,1,0:T(8,128)(2,1)S(1)}, bf16[1,1,2048,256]{3,2,1,0:T(8,128)(2,1)}, u32[]{:S(2)}) copy-start(bf16[1,1,2048,256]{3,2,1,0:T(8,128)(2,1)} %get-tuple-element.14) | copy-start | bytes 3145732
  315.8 7.3 %slice-start.5 = ((s8[6291456]{0:T(1024)(128)(4,1)}), s8[2097152]{0:T(1024)(128)(4,1)S(1)}, s32[]{:S(2)}) async-start(s8[6291456]{0:T(1024)(128)(4,1)} %bitcast.154), calls=%async_computation.20 | async-start | bytes 4194304
  322.7 1.0 copy-start.6
  322.7 1.2 copy-start.11
  322.7 1.4 copy-start.14
  322.7 1.5 copy-start.17
  322.8 1.7 copy-start.19
  329.5 68.5 %all-to-all-start.12 = ((f32[4,512,256]{2,1,0:T(8,128)}), f32[4,512,256]{2,1,0:T(8,128)S(1)}, u32[]{:S(2)}, u32[]{:S(2)}) async-start(f32[4,512,256]{2,1,0:T(8,128)} %broadcast_in_dim.27), calls=%async_computation.12 | async-start | bytes 4194304 | tf_op jit(solution)/shard_map/all_to_all | solution.py:49
  (1 other events, 0.8 us)
Sparse Core Ops, SparseCore 0:
  9.8 71.9 all-gather.4
  84.6 86.7 all-gather.6
where the time goes:
time: 410 us; the launch traced here: 409 us
  waiting for transfers between devices  202 us (49%)
  blocking collectives  117 us (29%)
  starting transfers between devices  35.7 us (9%)
  local copies, waits for them, and re-layouts  26.5 us (6%)
  between operations  14.6 us (4%)
  matrix products  10.9 us (3%)
    all_to_all x4, waiting for transfers between devices, sent_to_all(): return lax.all_to_all(copies, axis, split_axis=0, concat_axis=0, tiled=True)  91.7 us
    all_to_all x3, blocking collectives, sum_in_two_steps(): return jnp.sum(lax.all_to_all(own, far, 0, 0, tiled=True), axis=0)  81.9 us
    all_gather x1, waiting for transfers between devices, local(): gathered = lax.all_gather(activations[0], 'row', axis=1, tiled=True)  73.2 us
    all_to_all x4, starting transfers between devices, sent_to_all(): return lax.all_to_all(copies, axis, split_axis=0, concat_axis=0, tiled=True)  35.6 us
    all_gather x1, waiting for transfers between devices, local(): wanted_all = lax.all_gather(wanted_all, COL, axis=1, tiled=True)  35.4 us
    all_to_all x3, blocking collectives, sent_to_all(): return lax.all_to_all(copies, axis, split_axis=0, concat_axis=0, tiled=True)  18.6 us
    all_to_all x3, blocking collectives, summed_on_arrival(): parts = lax.all_to_all(split_up(shard, dim, count), axis, 0, 0, tiled=True)  16.6 us
  transfers between devices with their start and end apart: 6, of which 5 were waited for; matrix products, arithmetic and copies ran while one was open for 2% of the time, Pallas kernels for 0%

commit v1 on v0

v1 whole, which is shorter than its diff:
```python
import functools

import jax
import jax.numpy as jnp
from jax import lax
from jax.experimental import pallas as pl
from jax.experimental.pallas import tpu as pltpu
from jax.sharding import PartitionSpec as P

TOKENS = 2048
STEPS = 3
SLOW_STEPS = 1
PRIOR = 100
BLOCK = 512
PART = 128

beta_first = 0.9
beta_second = 0.95
inner_rate = 0.01
decay_rate = 0.1
epsilon_value = 1e-08
outer_rate = 0.7
momentum_coef = 0.9

F32 = jnp.float32
BF16 = jnp.bfloat16


def dot_nt(a, b):
    return lax.dot_general(a, b, (((1,), (1,)), ((), ())), preferred_element_type=F32)


def dot_nn(a, b):
    return lax.dot_general(a, b, (((1,), (0,)), ((), ())), preferred_element_type=F32)


def kernel(
    w_in, m_in, v_in, x_in, t_in, o_ref,
    xg, raw, wt, mt, vt, ot, wb, traw, own, ysend, yrecv, ysum, zsend, zrecv, resid, grad,
    dsend, drecv, pall, back, stage,
    lsem, xs, xr, ss, sr, ws, wr, ts, tr, ys, yr, zs, zr, gs, gr, ds_, dr, ps, pr, bs, br,
):
    g = lax.axis_index("grp")
    x = lax.axis_index("row")
    col = lax.axis_index("col")
    y = col // 4
    zh = (col // 2) % 2
    k = col % 2

    sib = {"col": col + 1 - 2 * k}
    zdev = {"col": y * 4 + (1 - zh) * 2 + k}
    right = {"row": (x + 1) % 4}
    left = {"row": (x + 3) % 4}
    xl, xr_, xo = (x + 3) % 4, (x + 1) % 4, (x + 2) % 4

    def ydev(j):
        return {"col": ((y + j) % 4) * 4 + zh * 2 + k}

    def gdev(j):
        return {"grp": (g + j) % 4}

    def quad(n):
        c = (zh * 2 + k + n) % 4
        return c, {"col": y * 4 + c}

    def remote(src, dst, s_sem, r_sem, dev):
        return pltpu.make_async_remote_copy(
            src_ref=src, dst_ref=dst, send_sem=s_sem, recv_sem=r_sem,
            device_id=dev, device_id_type=pl.DeviceIdType.MESH,
        )

    barrier = pltpu.get_barrier_semaphore()
    peers = [sib, right, left] + [ydev(j) for j in (1, 2, 3)]
    peers += [gdev(j) for j in (1, 2, 3)] + [quad(n)[1] for n in (1, 2, 3)]
    for dev in peers:
        pl.semaphore_signal(barrier, inc=1, device_id=dev, device_id_type=pl.DeviceIdType.MESH)

    mine = pl.ds(pl.multiple_of(k * PART, PART), PART)
    other = pl.ds(pl.multiple_of((1 - k) * PART, PART), PART)
    locals_ = [pltpu.make_async_copy(w_in.at[:, mine], raw.at[0, k], lsem.at[0])]
    locals_ += [pltpu.make_async_copy(x_in.at[0, s], xg.at[s, x, k], lsem.at[1 + s]) for s in range(STEPS)]
    locals_ += [pltpu.make_async_copy(m_in.at[0, :, mine], raw.at[1, k], lsem.at[4])]
    locals_ += [pltpu.make_async_copy(v_in.at[0, :, mine], raw.at[2, k], lsem.at[5])]
    me4 = zh * 2 + k
    locals_ += [pltpu.make_async_copy(t_in.at[0, :, :, mine], traw.at[me4], lsem.at[6])]
    for c in locals_:
        c.start()

    pl.semaphore_wait(barrier, len(peers))

    halves = (pl.ds(0, 256), pl.ds(256, 256))

    def x_own(s, h, way):
        return remote(
            x_in.at[0, s, halves[h]], xg.at[s, x, k, halves[h]],
            xs.at[s, 2 * way + h], xr.at[s, 2 * way + h], (right, left)[way],
        )

    def x_from(s, h, way):
        src = (xl, xr_)[way]
        return remote(
            xg.at[s, src, k, halves[h]], xg.at[s, src, k, halves[h]],
            xs.at[s, 2 * way + h], xr.at[s, 2 * way + h], (right, left)[way],
        )

    def x_fwd(s, way):
        src = (xl, xr_)[way]
        return remote(
            xg.at[s, src, k, halves[way]], xg.at[s, src, k, halves[way]],
            xs.at[s, 4 + way], xr.at[s, 4 + way], (right, left)[way],
        )

    def x_opp(s, way):
        return remote(
            xg.at[s, xo, k, halves[way]], xg.at[s, xo, k, halves[way]],
            xs.at[s, 4 + way], xr.at[s, 4 + way], (right, left)[way],
        )

    def x_sib(s, d, h, src=None):
        b = (x + d) % 4
        return remote(
            xg.at[s, b, k, halves[h]] if src is None else src, xg.at[s, b, k, halves[h]],
            ss.at[s, 2 * d + h], sr.at[s, 2 * d + h], sib,
        )

    def x_sib_in(s, d, h):
        b = (x + d) % 4
        return remote(
            xg.at[s, b, 1 - k, halves[h]], xg.at[s, b, 1 - k, halves[h]],
            ss.at[s, 2 * d + h], sr.at[s, 2 * d + h], sib,
        )

    def x_begin(s):
        x_own(s, 0, 0).start()
        x_own(s, 1, 1).start()
        x_own(s, 1, 0).start()
        x_own(s, 0, 1).start()
        for h in range(2):
            x_sib(s, 0, h, x_in.at[0, s, halves[h]]).start()

    def x_middle(s):
        x_from(s, 0, 0).wait_recv()
        x_fwd(s, 0).start()
        x_sib(s, 3, 0).start()
        x_from(s, 1, 1).wait_recv()
        x_fwd(s, 1).start()
        x_sib(s, 1, 1).start()
        x_from(s, 1, 0).wait_recv()
        x_sib(s, 3, 1).start()
        x_from(s, 0, 1).wait_recv()
        x_sib(s, 1, 0).start()

    def x_end(s):
        for way in range(2):
            x_opp(s, way).wait_recv()
            x_sib(s, 2, way).start()

    def swap(i, ref):
        return remote(ref, raw.at[i, k], ws.at[i], wr.at[i], sib)

    def swap_in(i):
        return remote(raw.at[i, 1 - k], raw.at[i, 1 - k], ws.at[i], wr.at[i], sib)

    def t_out(n):
        c, dev = quad(n)
        half = pl.ds(pl.multiple_of((c % 2) * PART, PART), PART)
        return remote(t_in.at[0, :, :, half], traw.at[me4], ts.at[n], tr.at[n], dev)

    def t_from(n):
        c, dev = quad(4 - n)
        return remote(traw.at[c], traw.at[c], ts.at[n], tr.at[n], dev)

    swap(0, w_in.at[:, other]).start()
    x_begin(0)
    swap(1, m_in.at[0, :, other]).start()
    swap(2, v_in.at[0, :, other]).start()
    for n in (1, 2, 3):
        t_out(n).start()

    def turned(i, dst):
        for kd in range(2):
            for r in range(4):
                dst[:, kd * BLOCK + r * PART : kd * BLOCK + (r + 1) * PART] = raw[
                    i, kd, r * PART : (r + 1) * PART, :
                ].T

    locals_[0].wait()
    swap_in(0).wait_recv()
    turned(0, wt)
    ot[...] = wt[...]
    wb[...] = wt[...].astype(BF16)
    locals_[4].wait()
    locals_[5].wait()
    swap_in(1).wait_recv()
    turned(1, mt)
    swap_in(2).wait_recv()
    turned(2, vt)

    def partial_of(s, b, q):
        rows = pl.ds(q * PART, PART)
        return dot_nt(wb[:, :BLOCK], xg[s, b, 0, rows, :]) + dot_nt(wb[:, BLOCK:], xg[s, b, 1, rows, :])

    def y_out(s, j, q):
        return remote(ysend.at[s, j, q], yrecv.at[s, j, q], ys.at[s, j, q], yr.at[s, j, q], ydev(j))

    def z_out(s, q):
        return remote(zsend.at[s, q], zrecv.at[s, q], zs.at[s, q], zr.at[s, q], zdev)

    def g_out(s, j, q):
        return remote(resid.at[s, y, q], resid.at[s, y, q], gs.at[s, j, q], gr.at[s, j, q], ydev(j))

    def g_from(s, j, q):
        b = (y + 4 - j) % 4
        return remote(resid.at[s, b, q], resid.at[s, b, q], gs.at[s, j, q], gr.at[s, j, q], ydev(j))

    def forward_block(s, b):
        j = (b + 4 - y) % 4
        for q in range(4):
            value = partial_of(s, b, q)

            @pl.when(j == 0)
            def _():
                own[q] = value

            @pl.when(j != 0)
            def _():
                ysend[s, j, q] = value.astype(BF16)
                y_out(s, j, q).start()

    def forward_pieces(s):
        for q in range(4):
            for j in (2, 1, 3):
                ysend[s, j, q] = partial_of(s, (y + j) % 4, q).astype(BF16)
                y_out(s, j, q).start()
            own[q] = partial_of(s, y, q)

    def middle(s):
        for q in range(4):
            total = own[q]
            for j in (1, 3, 2):
                y_out(s, j, q).wait_recv()
                total = total + yrecv[s, j, q].astype(F32)
            ysum[q] = total
            zsend[s, q] = total.astype(BF16)
            z_out(s, q).start()
        for q in range(4):
            wanted = traw[q, s].astype(F32).T
            z_out(s, q).wait_recv()
            output = ysum[q] + zrecv[s, q].astype(F32)
            resid[s, y, q] = (output - wanted).astype(BF16)
            for j in (2, 1, 3):
                g_out(s, j, q).start()

    def backward(s):
        r = jnp.concatenate([resid[s, y, q] for q in range(4)], axis=1)
        for kd in range(2):
            grad[:, kd * BLOCK : (kd + 1) * BLOCK] = dot_nn(r, xg[s, y, kd])
        for h in range(2):
            for j in (1, 3, 2):
                b = (y + 4 - j) % 4
                for q in (2 * h, 2 * h + 1):
                    g_from(s, j, q).wait_recv()
                r = jnp.concatenate([resid[s, b, 2 * h], resid[s, b, 2 * h + 1]], axis=1)
                for kd in range(2):
                    grad[:, kd * BLOCK : (kd + 1) * BLOCK] += dot_nn(r, xg[s, b, kd, halves[h], :])

    def update(s):
        power = PRIOR + s + 1

        @pl.loop(0, PART // 16)
        def _(i):
            rows = pl.ds(pl.multiple_of(i * 16, 16), 16)
            for cut in range(2):
                at = (rows, slice(cut * BLOCK, (cut + 1) * BLOCK))
                gradient = grad[at] * (1.0 / TOKENS)
                first = beta_first * mt[at] + (1.0 - beta_first) * gradient
                second = beta_second * vt[at] + (1.0 - beta_second) * gradient * gradient
                corrected = (
                    first
                    / (1.0 - beta_first**power)
                    / (jnp.sqrt(second / (1.0 - beta_second**power)) + epsilon_value)
                )
                old = wt[at]
                new = old - inner_rate * (corrected + decay_rate * old)
                mt[at] = first
                vt[at] = second
                wt[at] = new
                if s + 1 < STEPS:
                    wb[at] = new.astype(BF16)

    def x_arrived(s, d):
        for h in range(2):
            x_sib_in(s, d, h).wait_recv()

    locals_[1].wait()
    x_arrived(0, 0)
    forward_block(0, x)
    x_middle(0)
    x_arrived(0, 3)
    forward_block(0, xl)
    x_arrived(0, 1)
    forward_block(0, xr_)
    x_end(0)

    fast = g < 3

    @pl.when(fast)
    def _():
        x_begin(1)

    x_arrived(0, 2)
    forward_block(0, xo)
    locals_[6].wait()
    for n in (1, 2, 3):
        t_from(n).wait_recv()
    middle(0)

    @pl.when(fast)
    def _():
        x_middle(1)

    backward(0)
    update(0)

    locals_[2].wait()
    locals_[3].wait()

    @pl.when(fast)
    def _():
        for s in range(1, STEPS):
            x_end(s)
            if s + 1 < STEPS:
                x_begin(s + 1)
            for d in (0, 3, 1, 2):
                x_arrived(s, d)
            forward_pieces(s)
            middle(s)
            if s + 1 < STEPS:
                x_middle(s + 1)
            backward(s)
            update(s)

    weight = jnp.where(fast, float(STEPS), float(SLOW_STEPS)) / float(3 * STEPS + SLOW_STEPS)
    for i in range(4):
        cols = pl.ds(i * 256, 256)
        dsend[i] = weight * (ot[:, cols] - wt[:, cols])

    def d_out(j):
        return remote(dsend.at[(g + j) % 4], drecv.at[j], ds_.at[j], dr.at[j], gdev(j))

    def p_out(j):
        return remote(pall.at[g], pall.at[g], ps.at[j], pr.at[j], gdev(j))

    def p_from(j):
        c = (g + 4 - j) % 4
        return remote(pall.at[c], pall.at[c], ps.at[j], pr.at[j], gdev(j))

    for j in (2, 1, 3):
        d_out(j).start()
    total = dsend[g]
    for j in (1, 3, 2):
        d_out(j).wait_recv()
        total = total + drecv[j]
    pall[g] = total
    for j in (2, 1, 3):
        p_out(j).start()
    for j in (1, 3, 2):
        p_from(j).wait_recv()

    for i in range(4):
        for r in range(2):
            rows = slice((i % 2) * 256 + r * PART, (i % 2) * 256 + (r + 1) * PART)
            stage[i // 2, rows, :] = pall[i, :, r * PART : (r + 1) * PART].T
    away = remote(stage.at[1 - k], back, bs, br, sib)
    away.start()
    away.wait_recv()

    @pl.when(k == 0)
    def _():
        o_ref[:, :PART] = stage[0]
        o_ref[:, PART:] = back[...]

    @pl.when(k == 1)
    def _():
        o_ref[:, :PART] = back[...]
        o_ref[:, PART:] = stage[1]

    away.wait_send()
    for j in (1, 2, 3):
        d_out(j).wait_send()
        p_out(j).wait_send()
    for i in range(3):
        swap_in(i).wait_send()
    for n in (1, 2, 3):
        t_from(n).wait_send()

    def sent(s):
        for way in range(2):
            for h in range(2):
                x_own(s, h, way).wait_send()
            x_fwd(s, way).wait_send()
        for d in range(4):
            for h in range(2):
                x_sib(s, d, h).wait_send()
        for q in range(4):
            for j in (1, 2, 3):
                y_out(s, j, q).wait_send()
                g_out(s, j, q).wait_send()
            z_out(s, q).wait_send()

    sent(0)

    @pl.when(fast)
    def _():
        for s in range(1, STEPS):
            sent(s)


def pseudo_of(outer_params, first_moment, second_moment, activations, targets):
    dma = pltpu.SemaphoreType.DMA
    vm = pltpu.VMEM
    any_ = pl.BlockSpec(memory_space=pl.ANY)
    n = STEPS
    return pl.pallas_call(
        kernel,
        out_shape=jax.ShapeDtypeStruct((512, 256), F32),
        in_specs=[any_] * 5,
        out_specs=pl.BlockSpec(memory_space=pltpu.VMEM),
        scratch_shapes=[
            vm((n, 4, 2, 512, 512), BF16),
            vm((3, 2, 512, PART), F32),
            vm((PART, 1024), F32), vm((PART, 1024), F32), vm((PART, 1024), F32), vm((PART, 1024), F32),
            vm((PART, 1024), BF16),
            vm((4, n, PART, PART), BF16),
            vm((4, PART, PART), F32),
            vm((n, 4, 4, PART, PART), BF16), vm((n, 4, 4, PART, PART), BF16),
            vm((4, PART, PART), F32),
            vm((n, 4, PART, PART), BF16), vm((n, 4, PART, PART), BF16),
            vm((n, 4, 4, PART, PART), BF16),
            vm((PART, 1024), F32),
            vm((4, PART, 256), F32), vm((4, PART, 256), F32), vm((4, PART, 256), F32),
            vm((512, PART), F32),
            vm((2, 512, PART), F32),
            dma((7,)),
            dma((n, 6)), dma((n, 6)), dma((n, 8)), dma((n, 8)),
            dma((3,)), dma((3,)), dma((4,)), dma((4,)),
            dma((n, 4, 4)), dma((n, 4, 4)), dma((n, 4)), dma((n, 4)),
            dma((n, 4, 4)), dma((n, 4, 4)), dma((4,)), dma((4,)), dma((4,)), dma((4,)),
            dma, dma,
        ],
        compiler_params=pltpu.CompilerParams(
            collective_id=0, has_side_effects=True, vmem_limit_bytes=48 << 20
        ),
    )(outer_params, first_moment, second_moment, activations, targets)


def local(outer_params, first_moment, second_moment, outer_moment, activations, targets):
    pseudo = pseudo_of(outer_params, first_moment, second_moment, activations, targets)
    new_moment = momentum_coef * outer_moment + pseudo
    new_params = outer_params - outer_rate * (pseudo + momentum_coef * new_moment)
    return (new_params, new_moment)


def solution(mesh):
    placed = (
        P("col", "row"),
        P("grp", "col", "row"),
        P("grp", "col", "row"),
        P("col", "row"),
        P("grp", None, "row", "col"),
        P("grp", None, "col", "row"),
    )
    return jax.shard_map(
        local,
        mesh=mesh,
        in_specs=placed,
        out_specs=(P("col", "row"), P("col", "row")),
        check_vma=False,
    )
```

time: 410 us -> 133 us (0.32)
  waiting for transfers between devices: 202 us -> 0 us
  Pallas kernels: 0 us -> 125 us
  blocking collectives: 117 us -> 0 us
  starting transfers between devices: 35.7 us -> 0 us
  local copies, waits for them, and re-layouts: 26.5 us -> 5.45 us
  between operations: 14.6 us -> 0.66 us
  matrix products: 10.9 us -> 0 us
    pallas_call x0 -> x1, Pallas kernels: none -> 125 us  [pseudo_of(): pl.pallas_call(kernel, out_shape=jax.ShapeDtypeStruct((512, 256), F32), i...]
    all_to_all x9 -> x0, blocking collectives: 117 us -> none  [the longest x3 81.9 us: sum_in_two_steps(): return jnp.sum(lax.all_to_all(own, far, 0, 0, tiled=True), axis=0)]
    all_gather x2 -> x0, waiting for transfers between devices: 109 us -> none  [the longest x1 73.2 us: local(): gathered = lax.all_gather(activations[0], 'row', axis=1, tiled=True)]
    all_to_all x4 -> x0, waiting for transfers between devices: 91.7 us -> none  [sent_to_all(): return lax.all_to_all(copies, axis, split_axis=0, concat_axis=0, tiled=True)]
    all_to_all x4 -> x0, starting transfers between devices: 35.6 us -> none  [sent_to_all(): return lax.all_to_all(copies, axis, split_axis=0, concat_axis=0, tiled=True)]
    dot_general x6 -> x0, matrix products: 10.9 us -> none  [the longest x3 6.02 us: local(): jnp.dot(inputs, params.astype(jnp.bfloat16), preferred_element_type=jnp.f...]
    another operation x4 -> x0, local copies, waits for them, and re-layouts: 6.33 us -> none  [split_up(): return jnp.moveaxis(shard.reshape(*before, count, -1, *after), dim, 0)]
    broadcast_in_dim x7 -> x0, local copies, waits for them, and re-layouts: 5.3 us -> none  [sent_to_all(): copies = jnp.broadcast_to(shard, (lax.axis_size(axis), *shard.shape))]
  transfers between devices with their start and end apart: 6 -> 0, of which waited for: 5 -> 0; matrix products, arithmetic and copies ran while one was open for 2% -> 0% of each run, Pallas kernels for 0% -> 0%
where the time goes in v1:
time: 133 us
  Pallas kernels  125 us (94%)
  local copies, waits for them, and re-layouts  5.45 us (4%)
    pallas_call x1, Pallas kernels, pseudo_of(): pl.pallas_call(kernel, out_shape=jax.ShapeDtypeStruct((512, 256), F32), i...  125 us
    unnamed x12, local copies, waits for them, and re-layouts  5.45 us

profile of v1, /device:TPU:1, one launch (start us, length us, event | category | flops | bytes accessed | tf_op | source)
XLA Modules:
  0.0 132.6 jit_solution(13671814932414212377)
XLA Ops:
  0.6 0.0 copy-start
  0.6 1.0 copy-done
  1.7 0.0 copy-start.1
  1.7 1.4 %copy-done.1 = bf16[1,3,512,512]{3,2,1,0:T(8,128)(2,1)S(1)} copy-done((bf16[1,3,512,512]{3,2,1,0:T(8,128)(2,1)S(1)}, bf16[1,3,512,512]{3,2,1,0:T(8,128)(2,1)}, u32[]{:S(2)}) %copy-start.1) | copy-done | bytes 1572888
  3.1 0.0 copy-start.2
  3.1 1.0 copy-done.2
  4.1 0.0 copy-start.3
  4.1 1.0 copy-done.3
  5.2 0.0 copy-start.4
  5.2 0.9 copy-done.4
  6.1 0.0 copy-start.5
  6.1 125.4 %shard_map.77 = f32[512,256]{1,0:T(8,128)S(1)} custom-call(f32[512,256]{1,0:T(8,128)S(1)} %copy-done, f32[1,512,256]{2,1,0:T(8,128)S(1)} %copy-done.2, f32[1,512,256]{2,1,0:T(8,128)S(1)} %copy-done.3, bf16[1,3,512,512]{3,2,1,0:T(8,128)(2,1)S(1)} %copy-done.1, bf16[1,3,128,256]{3,2,1,0:T(8,128)(2,1)S(1)} %copy-done.4), custom_call_target="tpu_custom_call" | custom-call | tf_op jit(solution)/shard_map/pallas_call | solution.py:424
  131.5 0.0 copy-done.5
  131.5 1.1 multiply_subtract_fusion
Async XLA Ops:
  0.6 1.0 copy-start
  1.7 1.4 %copy-start.1 = (bf16[1,3,512,512]{3,2,1,0:T(8,128)(2,1)S(1)}, bf16[1,3,512,512]{3,2,1,0:T(8,128)(2,1)}, u32[]{:S(2)}) copy-start(bf16[1,3,512,512]{3,2,1,0:T(8,128)(2,1)} %x_in.1) | copy-start | bytes 4718596
  3.1 1.0 copy-start.2
  4.1 1.0 copy-start.3
  5.2 0.9 copy-start.4
  6.1 125.4 %copy-start.5 = (f32[512,256]{1,0:T(8,128)S(1)}, f32[512,256]{1,0:T(8,128)}, u32[]{:S(2)}) copy-start(f32[512,256]{1,0:T(8,128)} %param.9) | copy-start | bytes 1572868

commit v2 on v1

v2 whole, which is shorter than its diff:
```python
import functools

import jax
import jax.numpy as jnp
from jax import lax
from jax.experimental import pallas as pl
from jax.experimental.pallas import tpu as pltpu
from jax.sharding import PartitionSpec as P

TOKENS = 2048
STEPS = 3
SLOW_STEPS = 1
PRIOR = 100
BLOCK = 512
PART = 128

beta_first = 0.9
beta_second = 0.95
inner_rate = 0.01
decay_rate = 0.1
epsilon_value = 1e-08
outer_rate = 0.7
momentum_coef = 0.9

F32 = jnp.float32
BF16 = jnp.bfloat16


def dot_nt(a, b):
    return lax.dot_general(a, b, (((1,), (1,)), ((), ())), preferred_element_type=F32)


def dot_nn(a, b):
    return lax.dot_general(a, b, (((1,), (0,)), ((), ())), preferred_element_type=F32)


def kernel(
    w_in, m_in, v_in, x_in, t_in, o_ref,
    xg, raw, wt, mt, vt, ot, wb, traw, own, ysend, yrecv, ysum, zsend, zrecv, resid, grad,
    slow, slow_in, early, early_in, early_sum, left_over, late, late_in, late_sum, stage, back,
    lsem, xs, xr, ss, sr, ws, wr, ts, tr, ys, yr, zs, zr, gs, gr,
    os_, or_, es, er, as_, ar, ls, lr, fs, fr, bs, br,
):
    g = lax.axis_index("grp")
    x = lax.axis_index("row")
    col = lax.axis_index("col")
    y = col // 4
    zh = (col // 2) % 2
    k = col % 2

    def flip(g_, y_, zh_):
        return (y_ // 2 + zh_ + g_) % 2

    role = (k + flip(g, y, zh)) % 2

    def at(g_, y_, zh_):
        return {"grp": g_, "col": y_ * 4 + zh_ * 2 + (role + flip(g_, y_, zh_)) % 2}

    sib = {"col": y * 4 + zh * 2 + (1 - k)}
    zdev = at(g, y, 1 - zh)
    across = y * 4 + zh * 2 + (1 - k)
    right = {"row": (x + 1) % 4, "col": across}
    left = {"row": (x + 3) % 4, "col": across}
    xl, xr_, xo = (x + 3) % 4, (x + 1) % 4, (x + 2) % 4

    def ydev(j):
        return at(g, (y + j) % 4, zh)

    def gdev(j):
        return at((g + j) % 4, y, zh)

    def remote(src, dst, s_sem, r_sem, dev):
        return pltpu.make_async_remote_copy(
            src_ref=src, dst_ref=dst, send_sem=s_sem, recv_sem=r_sem,
            device_id=dev, device_id_type=pl.DeviceIdType.MESH,
        )

    barrier = pltpu.get_barrier_semaphore()
    peers = [sib, right, left, zdev] + [ydev(j) for j in (1, 2, 3)] + [gdev(j) for j in (1, 2, 3)]
    for dev in peers:
        pl.semaphore_signal(barrier, inc=1, device_id=dev, device_id_type=pl.DeviceIdType.MESH)

    mine = pl.ds(pl.multiple_of(role * PART, PART), PART)
    other = pl.ds(pl.multiple_of((1 - role) * PART, PART), PART)
    locals_ = [pltpu.make_async_copy(w_in.at[:, mine], raw.at[0, k], lsem.at[0])]
    locals_ += [pltpu.make_async_copy(x_in.at[0, s], xg.at[s, x, k], lsem.at[1 + s]) for s in range(STEPS)]
    locals_ += [pltpu.make_async_copy(m_in.at[0, :, mine], raw.at[1, k], lsem.at[4])]
    locals_ += [pltpu.make_async_copy(v_in.at[0, :, mine], raw.at[2, k], lsem.at[5])]
    locals_ += [pltpu.make_async_copy(t_in.at[0, :, :, mine], traw.at[k], lsem.at[6])]
    for c in locals_:
        c.start()

    pl.semaphore_wait(barrier, len(peers))

    halves = (pl.ds(0, 256), pl.ds(256, 256))

    def x_copy(s, slot, src, dst, way):
        return remote(src, dst, xs.at[s, slot], xr.at[s, slot], (right, left)[way])

    def x_own(s, h, way):
        return x_copy(s, 2 * way + h, x_in.at[0, s, halves[h]], xg.at[s, x, k, halves[h]], way)

    def x_from(s, h, way):
        here = xg.at[s, (xl, xr_)[way], 1 - k, halves[h]]
        return x_copy(s, 2 * way + h, here, here, way)

    def x_fwd(s, way):
        here = xg.at[s, (xl, xr_)[way], 1 - k, halves[way]]
        return x_copy(s, 4 + way, here, here, way)

    def x_opp(s, way):
        here = xg.at[s, xo, k, halves[way]]
        return x_copy(s, 4 + way, here, here, way)

    def x_sib(s, d, h, src=None, incoming=False):
        kd = (k + d + incoming) % 2
        here = xg.at[s, (x + d) % 4, kd, halves[h]]
        return remote(here if src is None else src, here, ss.at[s, 2 * d + h], sr.at[s, 2 * d + h], sib)

    def x_begin(s):
        x_own(s, 0, 0).start()
        x_own(s, 1, 1).start()
        x_own(s, 1, 0).start()
        x_own(s, 0, 1).start()
        for h in range(2):
            x_sib(s, 0, h, x_in.at[0, s, halves[h]]).start()

    def x_middle(s):
        x_from(s, 0, 0).wait_recv()
        x_fwd(s, 0).start()
        x_sib(s, 3, 0).start()
        x_from(s, 1, 1).wait_recv()
        x_fwd(s, 1).start()
        x_sib(s, 1, 1).start()
        x_from(s, 1, 0).wait_recv()
        x_sib(s, 3, 1).start()
        x_from(s, 0, 1).wait_recv()
        x_sib(s, 1, 0).start()

    def x_end(s):
        for way in range(2):
            x_opp(s, way).wait_recv()
            x_sib(s, 2, way).start()

    def swap(i, ref):
        return remote(ref, raw.at[i, k], ws.at[i], wr.at[i], sib)

    def swap_in(i):
        return remote(raw.at[i, 1 - k], raw.at[i, 1 - k], ws.at[i], wr.at[i], sib)

    def t_swap(kd):
        return remote(t_in.at[0, :, :, other], traw.at[kd], ts, tr, sib)

    swap(0, w_in.at[:, other]).start()
    x_begin(0)
    swap(1, m_in.at[0, :, other]).start()
    swap(2, v_in.at[0, :, other]).start()
    t_swap(k).start()

    def turned(i, dst):
        for kd in range(2):
            for r in range(4):
                dst[:, kd * BLOCK + r * PART : kd * BLOCK + (r + 1) * PART] = raw[
                    i, kd, r * PART : (r + 1) * PART, :
                ].T

    locals_[0].wait()
    swap_in(0).wait_recv()
    turned(0, wt)
    ot[...] = wt[...]
    wb[...] = wt[...].astype(BF16)
    locals_[4].wait()
    locals_[5].wait()
    swap_in(1).wait_recv()
    turned(1, mt)
    swap_in(2).wait_recv()
    turned(2, vt)

    def partial_of(s, b, q):
        rows = pl.ds(q * PART, PART)
        return dot_nt(wb[:, :BLOCK], xg[s, b, 0, rows, :]) + dot_nt(wb[:, BLOCK:], xg[s, b, 1, rows, :])

    def y_out(s, j, q):
        return remote(ysend.at[s, j, q], yrecv.at[s, j, q], ys.at[s, j, q], yr.at[s, j, q], ydev(j))

    def z_out(s, q):
        return remote(zsend.at[s, q], zrecv.at[s, q], zs.at[s, q], zr.at[s, q], zdev)

    def g_out(s, j, q):
        return remote(resid.at[s, y, q], resid.at[s, y, q], gs.at[s, j, q], gr.at[s, j, q], ydev(j))

    def g_from(s, j, q):
        b = (y + 4 - j) % 4
        return remote(resid.at[s, b, q], resid.at[s, b, q], gs.at[s, j, q], gr.at[s, j, q], ydev(j))

    def forward_block(s, b):
        j = (b + 4 - y) % 4
        for q in range(4):
            value = partial_of(s, b, q)

            @pl.when(j == 0)
            def _():
                own[q] = value

            @pl.when(j != 0)
            def _():
                ysend[s, j, q] = value.astype(BF16)
                y_out(s, j, q).start()

    def forward_pieces(s):
        for q in range(4):
            for j in (2, 1, 3):
                ysend[s, j, q] = partial_of(s, (y + j) % 4, q).astype(BF16)
                y_out(s, j, q).start()
            own[q] = partial_of(s, y, q)

    def middle(s):
        for kd in range(2):
            own[2 * zh + kd] = own[2 * zh + kd] - traw[kd, s].astype(F32).T
        for q in range(4):
            total = own[q]
            for j in (1, 3, 2):
                y_out(s, j, q).wait_recv()
                total = total + yrecv[s, j, q].astype(F32)
            ysum[q] = total
            zsend[s, q] = total.astype(BF16)
            z_out(s, q).start()
        for q in range(4):
            z_out(s, q).wait_recv()
            resid[s, y, q] = (ysum[q] + zrecv[s, q].astype(F32)).astype(BF16)
            for j in (2, 1, 3):
                g_out(s, j, q).start()

    def backward_own(s):
        r = jnp.concatenate([resid[s, y, q] for q in range(4)], axis=1)
        for kd in range(2):
            grad[:, kd * BLOCK : (kd + 1) * BLOCK] = dot_nn(r, xg[s, y, kd])

    def backward(s):
        for h in range(2):
            for j in (1, 3, 2):
                b = (y + 4 - j) % 4
                for q in (2 * h, 2 * h + 1):
                    g_from(s, j, q).wait_recv()
                r = jnp.concatenate([resid[s, b, 2 * h], resid[s, b, 2 * h + 1]], axis=1)
                for kd in range(2):
                    grad[:, kd * BLOCK : (kd + 1) * BLOCK] += dot_nn(r, xg[s, b, kd, halves[h], :])

    pieces = [(h, c) for c in range(4) for h in range(2)]

    def columns(h, c):
        return slice(h * BLOCK + c * PART, h * BLOCK + (c + 1) * PART)

    def update(s, then):
        power = PRIOR + s + 1
        for h, c in pieces:
            for cut in range(2):
                part = (slice(cut * 64, cut * 64 + 64), columns(h, c))
                gradient = grad[part] * (1.0 / TOKENS)
                first = beta_first * mt[part] + (1.0 - beta_first) * gradient
                second = beta_second * vt[part] + (1.0 - beta_second) * gradient * gradient
                corrected = (
                    first
                    / (1.0 - beta_first**power)
                    / (jnp.sqrt(second / (1.0 - beta_second**power)) + epsilon_value)
                )
                old = wt[part]
                new = old - inner_rate * (corrected + decay_rate * old)
                mt[part] = first
                vt[part] = second
                wt[part] = new
                if s + 1 < STEPS:
                    wb[part] = new.astype(BF16)
            then(h, c)

    def x_arrived(s, d):
        for h in range(2):
            x_sib(s, d, h, incoming=True).wait_recv()

    fast = g < 3
    total_steps = float(3 * STEPS + SLOW_STEPS)
    weight = jnp.where(fast, float(STEPS), float(SLOW_STEPS)) / total_steps

    def adder(h):
        return at(1 + h, y, zh)

    def slow_out(h):
        return remote(slow.at[h], slow_in, os_.at[h], or_, adder(h))

    way_in = jnp.where(g == 0, 0, 1)

    def early_out(h):
        return remote(early.at[h], early_in.at[way_in], es.at[h], er.at[way_in], adder(h))

    def early_from(i):
        return remote(early.at[0], early_in.at[i], es.at[0], er.at[i], adder(0))

    half = jnp.where(g == 2, 1, 0)
    adds = jnp.logical_or(g == 1, g == 2)

    def early_sum_out(j):
        return remote(early_sum.at[half], early_sum.at[half], as_.at[j], ar.at[half], gdev(j))

    def early_sum_from(h):
        return remote(early_sum.at[h], early_sum.at[h], as_.at[1], ar.at[h], gdev(1))

    def late_out(h, c):
        return remote(late.at[h, c], late_in.at[way_in, c], ls.at[h, c], lr.at[way_in, c], adder(h))

    def late_from(i, c):
        return remote(late.at[0, c], late_in.at[i, c], ls.at[0, c], lr.at[i, c], adder(0))

    def late_sum_out(j, c):
        return remote(late_sum.at[half, c], late_sum.at[half, c], fs.at[j, c], fr.at[half, c], gdev(j))

    def late_sum_from(h, c):
        return remote(late_sum.at[h, c], late_sum.at[h, c], fs.at[1, c], fr.at[h, c], gdev(1))

    def moved(h, c):
        return weight * (ot[:, columns(h, c)] - wt[:, columns(h, c)])

    def nothing(h, c):
        return None

    def to_slow(h, c):
        slow[h, c] = moved(h, c)

    def to_early(h, c):
        early[h, c] = moved(h, c).astype(BF16)
        if c == 3:

            @pl.when(g != 1 + h)
            def _():
                early_out(h).start()

    def to_late(h, c):
        late[h, c] = (moved(h, c) - early[h, c].astype(F32)).astype(BF16)

        @pl.when(g != 1 + h)
        def _():
            late_out(h, c).start()

    locals_[1].wait()
    x_arrived(0, 0)
    forward_block(0, x)
    x_middle(0)
    x_arrived(0, 3)
    forward_block(0, xl)
    x_arrived(0, 1)
    forward_block(0, xr_)
    x_end(0)

    @pl.when(fast)
    def _():
        x_begin(1)

    locals_[6].wait()
    t_swap(1 - k).wait_recv()
    x_arrived(0, 2)
    forward_block(0, xo)
    middle(0)

    @pl.when(fast)
    def _():
        x_middle(1)

    backward_own(0)
    backward(0)
    update(0, nothing)

    locals_[2].wait()
    locals_[3].wait()

    @pl.when(jnp.logical_not(fast))
    def _():
        for h, c in pieces:
            to_slow(h, c)
        for h in range(2):
            slow_out(h).start()

    @pl.when(fast)
    def _():
        for s in range(1, STEPS):
            x_end(s)
            if s + 1 < STEPS:
                x_begin(s + 1)
            for d in (0, 3, 1, 2):
                x_arrived(s, d)
            forward_pieces(s)
            middle(s)
            if s + 1 < STEPS:
                x_middle(s + 1)
            backward_own(s)
            if s + 1 == STEPS:

                @pl.when(adds)
                def _():
                    for i in range(2):
                        early_from(i).wait_recv()
                    slow_out(0).wait_recv()
                    for c in range(4):
                        total = early[half, c].astype(F32) + slow_in[c]
                        for i in range(2):
                            total = total + early_in[i, c].astype(F32)
                        rounded = total.astype(BF16)
                        early_sum[half, c] = rounded
                        left_over[c] = total - rounded.astype(F32)
                    for j in (2, 1, 3):
                        early_sum_out(j).start()

            backward(s)
            update(s, (nothing, to_early, to_late)[s])

    @pl.when(adds)
    def _():
        for c in range(4):
            total = late[half, c].astype(F32) + left_over[c]
            for i in range(2):
                late_from(i, c).wait_recv()
                total = total + late_in[i, c].astype(F32)
            late_sum[half, c] = total.astype(BF16)
            for j in (2, 1, 3):
                late_sum_out(j, c).start()

    for h in range(2):

        @pl.when(g != 1 + h)
        def _():
            early_sum_from(h).wait_recv()

    def away(c):
        return remote(stage.at[1 - k, c], back.at[c], bs.at[c], br.at[c], sib)

    for c in range(4):
        for h in range(2):

            @pl.when(g != 1 + h)
            def _():
                late_sum_from(h, c).wait_recv()

            stage[h, c] = (early_sum[h, c].astype(F32) + late_sum[h, c].astype(F32)).T
        away(c).start()
    for c in range(4):
        away(c).wait_recv()
        here = slice(c * PART, (c + 1) * PART)

        @pl.when(role == 0)
        def _():
            o_ref[here, :PART] = stage[k, c]
            o_ref[here, PART:] = back[c]

        @pl.when(role == 1)
        def _():
            o_ref[here, :PART] = back[c]
            o_ref[here, PART:] = stage[k, c]

    for c in range(4):
        away(c).wait_send()
    for i in range(3):
        swap_in(i).wait_send()
    t_swap(k).wait_send()

    @pl.when(adds)
    def _():
        for j in (1, 2, 3):
            early_sum_out(j).wait_send()
            for c in range(4):
                late_sum_out(j, c).wait_send()

    def sent(s):
        for way in range(2):
            for h in range(2):
                x_own(s, h, way).wait_send()
            x_fwd(s, way).wait_send()
        for d in range(4):
            for h in range(2):
                x_sib(s, d, h).wait_send()
        for q in range(4):
            for j in (1, 2, 3):
                y_out(s, j, q).wait_send()
                g_out(s, j, q).wait_send()
            z_out(s, q).wait_send()

    sent(0)

    @pl.when(jnp.logical_not(fast))
    def _():
        for h in range(2):
            slow_out(h).wait_send()

    @pl.when(fast)
    def _():
        for s in range(1, STEPS):
            sent(s)
        for h in range(2):

            @pl.when(g != 1 + h)
            def _():
                early_out(h).wait_send()
                for c in range(4):
                    late_out(h, c).wait_send()


def pseudo_of(outer_params, first_moment, second_moment, activations, targets):
    dma = pltpu.SemaphoreType.DMA
    vm = pltpu.VMEM
    hbm = pl.BlockSpec(memory_space=pltpu.HBM)
    n = STEPS
    tile = (PART, PART)
    return pl.pallas_call(
        kernel,
        out_shape=jax.ShapeDtypeStruct((512, 256), F32),
        in_specs=[hbm] * 5,
        out_specs=pl.BlockSpec(memory_space=pltpu.VMEM),
        scratch_shapes=[
            vm((n, 4, 2, 512, 512), BF16),
            vm((3, 2, 512, PART), F32),
            vm((PART, 1024), F32), vm((PART, 1024), F32), vm((PART, 1024), F32), vm((PART, 1024), F32),
            vm((PART, 1024), BF16),
            vm((2, n, *tile), BF16),
            vm((4, *tile), F32),
            vm((n, 4, 4, *tile), BF16), vm((n, 4, 4, *tile), BF16),
            vm((4, *tile), F32),
            vm((n, 4, *tile), BF16), vm((n, 4, *tile), BF16),
            vm((n, 4, 4, *tile), BF16),
            vm((PART, 1024), F32),
            vm((2, 4, *tile), F32), vm((4, *tile), F32),
            vm((2, 4, *tile), BF16), vm((2, 4, *tile), BF16), vm((2, 4, *tile), BF16),
            vm((4, *tile), F32),
            vm((2, 4, *tile), BF16), vm((2, 4, *tile), BF16), vm((2, 4, *tile), BF16),
            vm((2, 4, *tile), F32), vm((4, *tile), F32),
            dma((7,)),
            dma((n, 6)), dma((n, 6)), dma((n, 8)), dma((n, 8)),
            dma((3,)), dma((3,)), dma, dma,
            dma((n, 4, 4)), dma((n, 4, 4)), dma((n, 4)), dma((n, 4)),
            dma((n, 4, 4)), dma((n, 4, 4)),
            dma((2,)), dma, dma((2,)), dma((2,)), dma((4,)), dma((2,)),
            dma((2, 4)), dma((2, 4)), dma((4, 4)), dma((2, 4)),
            dma((4,)), dma((4,)),
        ],
        compiler_params=pltpu.CompilerParams(
            collective_id=0, has_side_effects=True, vmem_limit_bytes=63 << 20
        ),
    )(outer_params, first_moment, second_moment, activations, targets)


def local(outer_params, first_moment, second_moment, outer_moment, activations, targets):
    pseudo = pseudo_of(outer_params, first_moment, second_moment, activations, targets)
    new_moment = momentum_coef * outer_moment + pseudo
    new_params = outer_params - outer_rate * (pseudo + momentum_coef * new_moment)
    return (new_params, new_moment)


def solution(mesh):
    placed = (
        P("col", "row"),
        P("grp", "col", "row"),
        P("grp", "col", "row"),
        P("col", "row"),
        P("grp", None, "row", "col"),
        P("grp", None, "col", "row"),
    )
    return jax.shard_map(
        local,
        mesh=mesh,
        in_specs=placed,
        out_specs=(P("col", "row"), P("col", "row")),
        check_vma=False,
    )
```

time: 133 us -> 118 us (0.89)
  Pallas kernels: 125 us -> 115 us
  local copies, waits for them, and re-layouts: 5.45 us -> 0.01 us
    pallas_call x1, Pallas kernels: 125 us -> 115 us  [pseudo_of(): pl.pallas_call(kernel, out_shape=jax.ShapeDtypeStruct((512, 256), F32), i...]
    unnamed x12 -> x2, local copies, waits for them, and re-layouts: 5.45 us -> 0.01 us
where the time goes in v2:
time: 118 us
  Pallas kernels  115 us (97%)
  other arithmetic  2.29 us (2%)
    pallas_call x1, Pallas kernels, pseudo_of(): pl.pallas_call(kernel, out_shape=jax.ShapeDtypeStruct((512, 256), F32), i...  115 us

profile of v2, /device:TPU:1, one launch (start us, length us, event | category | flops | bytes accessed | tf_op | source)
XLA Modules:
  0.0 118.3 jit_solution(6033981601963637453)
XLA Ops:
  0.6 0.0 copy-start
  0.6 115.4 %shard_map.77 = f32[512,256]{1,0:T(8,128)} custom-call(f32[512,256]{1,0:T(8,128)} %w_in.1, f32[1,512,256]{2,1,0:T(8,128)} %m_in.1, f32[1,512,256]{2,1,0:T(8,128)} %v_in.1, bf16[1,3,512,512]{3,2,1,0:T(8,128)(2,1)} %x_in.1, bf16[1,3,128,256]{3,2,1,0:T(8,128)(2,1)} %t_in.1), custom_call_target="tpu_custom_call" | custom-call | tf_op jit(solution)/shard_map/pallas_call | solution.py:510
  116.0 0.0 copy-done
  116.1 2.3 %multiply_subtract_fusion = (f32[512,256]{1,0:T(8,128)}, f32[512,256]{1,0:T(8,128)}) fusion(f32[512,256]{1,0:T(8,128)S(1)} %copy-done, f32[512,256]{1,0:T(8,128)} %shard_map.77, f32[512,256]{1,0:T(8,128)} %param.9), kind=kLoop, calls=%fused_computation | loop fusion | flops 786432 | bytes 2621440 | tf_op jit(solution)/shard_map/sub | solution.py:550
Async XLA Ops:
  0.6 115.4 %copy-start = (f32[512,256]{1,0:T(8,128)S(1)}, f32[512,256]{1,0:T(8,128)}, u32[]{:S(2)}) copy-start(f32[512,256]{1,0:T(8,128)} %w_in.1) | copy-start | bytes 1572868

commit v3 on v2

--- a/solution.py
+++ b/solution.py
@@ -13,6 +13,7 @@
 PRIOR = 100
 BLOCK = 512
 PART = 128
+CUTS = (1, 1, 1, 1)
 
 beta_first = 0.9
 beta_second = 0.95
@@ -132,6 +133,8 @@
         x_from(s, 1, 1).wait_recv()
         x_fwd(s, 1).start()
         x_sib(s, 1, 1).start()
+
+    def x_rest(s):
         x_from(s, 1, 0).wait_recv()
         x_sib(s, 3, 1).start()
         x_from(s, 0, 1).wait_recv()
@@ -180,18 +183,26 @@
         rows = pl.ds(q * PART, PART)
         return dot_nt(wb[:, :BLOCK], xg[s, b, 0, rows, :]) + dot_nt(wb[:, BLOCK:], xg[s, b, 1, rows, :])
 
-    def y_out(s, j, q):
-        return remote(ysend.at[s, j, q], yrecv.at[s, j, q], ys.at[s, j, q], yr.at[s, j, q], ydev(j))
-
-    def z_out(s, q):
-        return remote(zsend.at[s, q], zrecv.at[s, q], zs.at[s, q], zr.at[s, q], zdev)
-
-    def g_out(s, j, q):
-        return remote(resid.at[s, y, q], resid.at[s, y, q], gs.at[s, j, q], gr.at[s, j, q], ydev(j))
-
-    def g_from(s, j, q):
-        b = (y + 4 - j) % 4
-        return remote(resid.at[s, b, q], resid.at[s, b, q], gs.at[s, j, q], gr.at[s, j, q], ydev(j))
+    def cuts(q):
+        height = PART // CUTS[q]
+        return [(i, slice(i * height, (i + 1) * height)) for i in range(CUTS[q])]
+
+    def y_out(s, j, q, i, rows):
+        here, there = ysend.at[s, j, q, rows], yrecv.at[s, j, q, rows]
+        return remote(here, there, ys.at[s, j, q, i], yr.at[s, j, q, i], ydev(j))
+
+    def z_out(s, q, i, rows):
+        return remote(zsend.at[s, q, rows], zrecv.at[s, q, rows], zs.at[s, q, i], zr.at[s, q, i], zdev)
+
+    def g_copy(s, b, j, q, i, rows):
+        here = resid.at[s, b, q, rows]
+        return remote(here, here, gs.at[s, j, q, i], gr.at[s, j, q, i], ydev(j))
+
+    def g_out(s, j, q, i, rows):
+        return g_copy(s, y, j, q, i, rows)
+
+    def g_from(s, j, q, i, rows):
+        return g_copy(s, (y + 4 - j) % 4, j, q, i, rows)
 
     def forward_block(s, b):
         j = (b + 4 - y) % 4
@@ -205,31 +216,39 @@
             @pl.when(j != 0)
             def _():
                 ysend[s, j, q] = value.astype(BF16)
-                y_out(s, j, q).start()
+                for cut in cuts(q):
+                    y_out(s, j, q, *cut).start()
 
     def forward_pieces(s):
         for q in range(4):
             for j in (2, 1, 3):
                 ysend[s, j, q] = partial_of(s, (y + j) % 4, q).astype(BF16)
-                y_out(s, j, q).start()
+                y_out(s, j, q, *cuts(q)[0]).start()
+            for cut in cuts(q)[1:]:
+                for j in (2, 1, 3):
+                    y_out(s, j, q, *cut).start()
             own[q] = partial_of(s, y, q)
 
-    def middle(s):
+    def gather_y(s):
         for kd in range(2):
             own[2 * zh + kd] = own[2 * zh + kd] - traw[kd, s].astype(F32).T
         for q in range(4):
-            total = own[q]
-            for j in (1, 3, 2):
-                y_out(s, j, q).wait_recv()
-                total = total + yrecv[s, j, q].astype(F32)
-            ysum[q] = total
-            zsend[s, q] = total.astype(BF16)
-            z_out(s, q).start()
+            for i, rows in cuts(q):
+                total = own[q, rows]
+                for j in (1, 3, 2):
+                    y_out(s, j, q, i, rows).wait_recv()
+                    total = total + yrecv[s, j, q, rows].astype(F32)
+                ysum[q, rows] = total
+                zsend[s, q, rows] = total.astype(BF16)
+                z_out(s, q, i, rows).start()
+
+    def gather_z(s):
         for q in range(4):
-            z_out(s, q).wait_recv()
-            resid[s, y, q] = (ysum[q] + zrecv[s, q].astype(F32)).astype(BF16)
-            for j in (2, 1, 3):
-                g_out(s, j, q).start()
+            for i, rows in cuts(q):
+                z_out(s, q, i, rows).wait_recv()
+                resid[s, y, q, rows] = (ysum[q, rows] + zrecv[s, q, rows].astype(F32)).astype(BF16)
+                for j in (2, 1, 3):
+                    g_out(s, j, q, i, rows).start()
 
     def backward_own(s):
         r = jnp.concatenate([resid[s, y, q] for q in range(4)], axis=1)
@@ -241,7 +260,8 @@
             for j in (1, 3, 2):
                 b = (y + 4 - j) % 4
                 for q in (2 * h, 2 * h + 1):
-                    g_from(s, j, q).wait_recv()
+                    for cut in cuts(q):
+                        g_from(s, j, q, *cut).wait_recv()
                 r = jnp.concatenate([resid[s, b, 2 * h], resid[s, b, 2 * h + 1]], axis=1)
                 for kd in range(2):
                     grad[:, kd * BLOCK : (kd + 1) * BLOCK] += dot_nn(r, xg[s, b, kd, halves[h], :])
@@ -277,6 +297,21 @@
         for h in range(2):
             x_sib(s, d, h, incoming=True).wait_recv()
 
+    def sent(s):
+        for way in range(2):
+            for h in range(2):
+                x_own(s, h, way).wait_send()
+            x_fwd(s, way).wait_send()
+        for d in range(4):
+            for h in range(2):
+                x_sib(s, d, h).wait_send()
+        for q in range(4):
+            for cut in cuts(q):
+                for j in (1, 2, 3):
+                    y_out(s, j, q, *cut).wait_send()
+                    g_out(s, j, q, *cut).wait_send()
+                z_out(s, q, *cut).wait_send()
+
     fast = g < 3
     total_steps = float(3 * STEPS + SLOW_STEPS)
     weight = jnp.where(fast, float(STEPS), float(SLOW_STEPS)) / total_steps
@@ -344,27 +379,34 @@
     x_arrived(0, 0)
     forward_block(0, x)
     x_middle(0)
+    x_rest(0)
     x_arrived(0, 3)
     forward_block(0, xl)
     x_arrived(0, 1)
     forward_block(0, xr_)
+
+    @pl.when(fast)
+    def _():
+        x_begin(1)
+
     x_end(0)
-
-    @pl.when(fast)
-    def _():
-        x_begin(1)
-
     locals_[6].wait()
     t_swap(1 - k).wait_recv()
     x_arrived(0, 2)
     forward_block(0, xo)
-    middle(0)
+    gather_y(0)
 
     @pl.when(fast)
     def _():
         x_middle(1)
 
+    gather_z(0)
     backward_own(0)
+
+    @pl.when(fast)
+    def _():
+        x_rest(1)
+
     backward(0)
     update(0, nothing)
 
@@ -377,6 +419,12 @@
             to_slow(h, c)
         for h in range(2):
             slow_out(h).start()
+        sent(0)
+        for i in range(3):
+            swap_in(i).wait_send()
+        t_swap(k).wait_send()
+        for h in range(2):
+            slow_out(h).wait_send()
 
     @pl.when(fast)
     def _():
@@ -387,10 +435,18 @@
             for d in (0, 3, 1, 2):
                 x_arrived(s, d)
             forward_pieces(s)
-            middle(s)
+            sent(s - 1)
+            if s == 1:
+                for i in range(3):
+                    swap_in(i).wait_send()
+                t_swap(k).wait_send()
+            gather_y(s)
             if s + 1 < STEPS:
                 x_middle(s + 1)
+            gather_z(s)
             backward_own(s)
+            if s + 1 < STEPS:
+                x_rest(s + 1)
             if s + 1 == STEPS:
 
                 @pl.when(adds)
@@ -422,6 +478,22 @@
             for j in (2, 1, 3):
                 late_sum_out(j, c).start()
 
+    @pl.when(fast)
+    def _():
+        sent(STEPS - 1)
+        for h in range(2):
+
+            @pl.when(g != 1 + h)
+            def _():
+                early_out(h).wait_send()
+                for c in range(4):
+                    late_out(h, c).wait_send()
+
+    @pl.when(adds)
+    def _():
+        for j in (1, 2, 3):
+            early_sum_out(j).wait_send()
+
     for h in range(2):
 
         @pl.when(g != 1 + h)
@@ -456,49 +528,12 @@
 
     for c in range(4):
         away(c).wait_send()
-    for i in range(3):
-        swap_in(i).wait_send()
-    t_swap(k).wait_send()
 
     @pl.when(adds)
     def _():
         for j in (1, 2, 3):
-            early_sum_out(j).wait_send()
             for c in range(4):
                 late_sum_out(j, c).wait_send()
-
-    def sent(s):
-        for way in range(2):
-            for h in range(2):
-                x_own(s, h, way).wait_send()
-            x_fwd(s, way).wait_send()
-        for d in range(4):
-            for h in range(2):
-                x_sib(s, d, h).wait_send()
-        for q in range(4):
-            for j in (1, 2, 3):
-                y_out(s, j, q).wait_send()
-                g_out(s, j, q).wait_send()
-            z_out(s, q).wait_send()
-
-    sent(0)
-
-    @pl.when(jnp.logical_not(fast))
-    def _():
-        for h in range(2):
-            slow_out(h).wait_send()
-
-    @pl.when(fast)
-    def _():
-        for s in range(1, STEPS):
-            sent(s)
-        for h in range(2):
-
-            @pl.when(g != 1 + h)
-            def _():
-                early_out(h).wait_send()
-                for c in range(4):
-                    late_out(h, c).wait_send()
 
 
 def pseudo_of(outer_params, first_moment, second_moment, activations, targets):
@@ -532,8 +567,8 @@
             dma((7,)),
             dma((n, 6)), dma((n, 6)), dma((n, 8)), dma((n, 8)),
             dma((3,)), dma((3,)), dma, dma,
-            dma((n, 4, 4)), dma((n, 4, 4)), dma((n, 4)), dma((n, 4)),
-            dma((n, 4, 4)), dma((n, 4, 4)),
+            dma((n, 4, 4, max(CUTS))), dma((n, 4, 4, max(CUTS))), dma((n, 4, max(CUTS))), dma((n, 4, max(CUTS))),
+            dma((n, 4, 4, max(CUTS))), dma((n, 4, 4, max(CUTS))),
             dma((2,)), dma, dma((2,)), dma((2,)), dma((4,)), dma((2,)),
             dma((2, 4)), dma((2, 4)), dma((4, 4)), dma((2, 4)),
             dma((4,)), dma((4,)),

time: 118 us -> 113 us (0.958)
  Pallas kernels: 115 us -> 110 us
    pallas_call x1, Pallas kernels: 115 us -> 110 us  [pseudo_of(): pl.pallas_call(kernel, out_shape=jax.ShapeDtypeStruct((512, 256), F32), i...]
where the time goes in v3:
time: 113 us
  Pallas kernels  110 us (97%)
  other arithmetic  2.29 us (2%)
    pallas_call x1, Pallas kernels, pseudo_of(): pl.pallas_call(kernel, out_shape=jax.ShapeDtypeStruct((512, 256), F32), i...  110 us
    sub x1, other arithmetic, local(): outer_params - outer_rate * (pseudo + momentum_coef * new_moment)  2.29 us

profile of v3, /device:TPU:1, one launch (start us, length us, event | category | flops | bytes accessed | tf_op | source)
XLA Modules:
  0.0 112.7 jit_solution(8638065783497502474)
XLA Ops:
  0.6 0.0 copy-start
  0.6 109.8 %shard_map.77 = f32[512,256]{1,0:T(8,128)} custom-call(f32[512,256]{1,0:T(8,128)} %w_in.1, f32[1,512,256]{2,1,0:T(8,128)} %m_in.1, f32[1,512,256]{2,1,0:T(8,128)} %v_in.1, bf16[1,3,512,512]{3,2,1,0:T(8,128)(2,1)} %x_in.1, bf16[1,3,128,256]{3,2,1,0:T(8,128)(2,1)} %t_in.1), custom_call_target="tpu_custom_call" | custom-call | tf_op jit(solution)/shard_map/pallas_call | solution.py:545
  110.4 0.0 copy-done
  110.4 2.3 %multiply_subtract_fusion = (f32[512,256]{1,0:T(8,128)}, f32[512,256]{1,0:T(8,128)}) fusion(f32[512,256]{1,0:T(8,128)S(1)} %copy-done, f32[512,256]{1,0:T(8,128)} %shard_map.77, f32[512,256]{1,0:T(8,128)} %param.9), kind=kLoop, calls=%fused_computation | loop fusion | flops 786432 | bytes 2621440 | tf_op jit(solution)/shard_map/sub | solution.py:585
Async XLA Ops:
  0.6 109.8 %copy-start = (f32[512,256]{1,0:T(8,128)S(1)}, f32[512,256]{1,0:T(8,128)}, u32[]{:S(2)}) copy-start(f32[512,256]{1,0:T(8,128)} %w_in.1) | copy-start | bytes 1572868

commit v4 on v3

--- a/solution.py
+++ b/solution.py
@@ -13,7 +13,6 @@
 PRIOR = 100
 BLOCK = 512
 PART = 128
-CUTS = (1, 1, 1, 1)
 
 beta_first = 0.9
 beta_second = 0.95
@@ -67,6 +66,9 @@
     def ydev(j):
         return at(g, (y + j) % 4, zh)
 
+    def core_of(role_, y_):
+        return {"col": y_ * 4 + zh * 2 + (role_ + flip(g, y_, zh)) % 2}
+
     def gdev(j):
         return at((g + j) % 4, y, zh)
 
@@ -78,6 +80,7 @@
 
     barrier = pltpu.get_barrier_semaphore()
     peers = [sib, right, left, zdev] + [ydev(j) for j in (1, 2, 3)] + [gdev(j) for j in (1, 2, 3)]
+    peers += [core_of(1 - role, (y + j) % 4) for j in (1, 2, 3)]
     for dev in peers:
         pl.semaphore_signal(barrier, inc=1, device_id=dev, device_id_type=pl.DeviceIdType.MESH)
 
@@ -87,7 +90,6 @@
     locals_ += [pltpu.make_async_copy(x_in.at[0, s], xg.at[s, x, k], lsem.at[1 + s]) for s in range(STEPS)]
     locals_ += [pltpu.make_async_copy(m_in.at[0, :, mine], raw.at[1, k], lsem.at[4])]
     locals_ += [pltpu.make_async_copy(v_in.at[0, :, mine], raw.at[2, k], lsem.at[5])]
-    locals_ += [pltpu.make_async_copy(t_in.at[0, :, :, mine], traw.at[k], lsem.at[6])]
     for c in locals_:
         c.start()
 
@@ -151,14 +153,42 @@
     def swap_in(i):
         return remote(raw.at[i, 1 - k], raw.at[i, 1 - k], ws.at[i], wr.at[i], sib)
 
-    def t_swap(kd):
-        return remote(t_in.at[0, :, :, other], traw.at[kd], ts, tr, sib)
+    t_owner = zh * 2 + k
+
+    def t_out(r):
+        here = t_in.at[0, :, :, slice(r * PART, (r + 1) * PART)]
+        return remote(here, traw.at[y], ts.at[r], tr.at[y], core_of(r, t_owner))
+
+    def t_stays(r):
+        return jnp.logical_and(t_owner == y, role == r)
+
+    t_local = pltpu.make_async_copy(t_in.at[0, :, :, mine], traw.at[y], lsem.at[6])
+    holds = zh == y // 2
+
+    def t_from(b):
+        return remote(traw.at[b], traw.at[b], ts.at[0], tr.at[b], sib)
+
+    def t_sent():
+        for r in range(2):
+
+            @pl.when(jnp.logical_not(t_stays(r)))
+            def _():
+                t_out(r).wait_send()
 
     swap(0, w_in.at[:, other]).start()
     x_begin(0)
     swap(1, m_in.at[0, :, other]).start()
     swap(2, v_in.at[0, :, other]).start()
-    t_swap(k).start()
+    for r in range(2):
+
+        @pl.when(t_stays(r))
+        def _():
+            t_local.start()
+
+        @pl.when(jnp.logical_not(t_stays(r)))
+        def _():
+            t_out(r).start()
+
 
     def turned(i, dst):
         for kd in range(2):
@@ -179,92 +209,76 @@
     swap_in(2).wait_recv()
     turned(2, vt)
 
-    def partial_of(s, b, q):
-        rows = pl.ds(q * PART, PART)
+    blocks = (x, xl, xr_, xo)
+    order = (0, 3, 1, 2)
+
+    def quarter(y_):
+        return pl.ds(pl.multiple_of(y_ * PART, PART), PART)
+
+    def partial_of(s, p, y_):
+        b, rows = blocks[p], quarter(y_)
         return dot_nt(wb[:, :BLOCK], xg[s, b, 0, rows, :]) + dot_nt(wb[:, BLOCK:], xg[s, b, 1, rows, :])
 
-    def cuts(q):
-        height = PART // CUTS[q]
-        return [(i, slice(i * height, (i + 1) * height)) for i in range(CUTS[q])]
-
-    def y_out(s, j, q, i, rows):
-        here, there = ysend.at[s, j, q, rows], yrecv.at[s, j, q, rows]
-        return remote(here, there, ys.at[s, j, q, i], yr.at[s, j, q, i], ydev(j))
-
-    def z_out(s, q, i, rows):
-        return remote(zsend.at[s, q, rows], zrecv.at[s, q, rows], zs.at[s, q, i], zr.at[s, q, i], zdev)
-
-    def g_copy(s, b, j, q, i, rows):
-        here = resid.at[s, b, q, rows]
-        return remote(here, here, gs.at[s, j, q, i], gr.at[s, j, q, i], ydev(j))
-
-    def g_out(s, j, q, i, rows):
-        return g_copy(s, y, j, q, i, rows)
-
-    def g_from(s, j, q, i, rows):
-        return g_copy(s, (y + 4 - j) % 4, j, q, i, rows)
-
-    def forward_block(s, b):
-        j = (b + 4 - y) % 4
-        for q in range(4):
-            value = partial_of(s, b, q)
-
-            @pl.when(j == 0)
-            def _():
-                own[q] = value
-
-            @pl.when(j != 0)
-            def _():
-                ysend[s, j, q] = value.astype(BF16)
-                for cut in cuts(q):
-                    y_out(s, j, q, *cut).start()
-
-    def forward_pieces(s):
-        for q in range(4):
-            for j in (2, 1, 3):
-                ysend[s, j, q] = partial_of(s, (y + j) % 4, q).astype(BF16)
-                y_out(s, j, q, *cuts(q)[0]).start()
-            for cut in cuts(q)[1:]:
-                for j in (2, 1, 3):
-                    y_out(s, j, q, *cut).start()
-            own[q] = partial_of(s, y, q)
-
-    def gather_y(s):
+    def y_out(s, j, p):
+        return remote(ysend.at[s, j, p], yrecv.at[s, j, p], ys.at[s, j, p], yr.at[s, j, p], ydev(j))
+
+    def z_out(s, p):
+        return remote(zsend.at[s, p], zrecv.at[s, p], zs.at[s, p], zr.at[s, p], zdev)
+
+    def g_copy(s, y_, j, p):
+        here = resid.at[s, y_, p]
+        return remote(here, here, gs.at[s, j, p], gr.at[s, j, p], ydev(j))
+
+    def g_out(s, j, p):
+        return g_copy(s, y, j, p)
+
+    def g_from(s, j, p):
+        return g_copy(s, (y + 4 - j) % 4, j, p)
+
+    def forward(s, p):
+        for h in range(2):
+            x_sib(s, order[p], h, incoming=True).wait_recv()
+        for j in (2, 1, 3):
+            ysend[s, j, p] = partial_of(s, p, (y + j) % 4).astype(BF16)
+            y_out(s, j, p).start()
+        own[p] = partial_of(s, p, y)
+
+    def gather_y(s, p):
+        @pl.when(holds)
+        def _():
+            own[p] = own[p] - traw[blocks[p], s].astype(F32).T
+
+        total = own[p]
+        for j in (1, 3, 2):
+            y_out(s, j, p).wait_recv()
+            total = total + yrecv[s, j, p].astype(F32)
+        ysum[p] = total
+        zsend[s, p] = total.astype(BF16)
+        z_out(s, p).start()
+
+    def gather_z(s, p):
+        z_out(s, p).wait_recv()
+        resid[s, y, p] = (ysum[p] + zrecv[s, p].astype(F32)).astype(BF16)
+        for j in (2, 1, 3):
+            g_out(s, j, p).start()
+
+    def rows_of(s, kd, y_, ps):
+        return jnp.concatenate([xg[s, blocks[p], kd, quarter(y_), :] for p in ps], axis=0)
+
+    def backward_own(s):
+        r = jnp.concatenate([resid[s, y, p] for p in range(4)], axis=1)
         for kd in range(2):
-            own[2 * zh + kd] = own[2 * zh + kd] - traw[kd, s].astype(F32).T
-        for q in range(4):
-            for i, rows in cuts(q):
-                total = own[q, rows]
-                for j in (1, 3, 2):
-                    y_out(s, j, q, i, rows).wait_recv()
-                    total = total + yrecv[s, j, q, rows].astype(F32)
-                ysum[q, rows] = total
-                zsend[s, q, rows] = total.astype(BF16)
-                z_out(s, q, i, rows).start()
-
-    def gather_z(s):
-        for q in range(4):
-            for i, rows in cuts(q):
-                z_out(s, q, i, rows).wait_recv()
-                resid[s, y, q, rows] = (ysum[q, rows] + zrecv[s, q, rows].astype(F32)).astype(BF16)
-                for j in (2, 1, 3):
-                    g_out(s, j, q, i, rows).start()
-
-    def backward_own(s):
-        r = jnp.concatenate([resid[s, y, q] for q in range(4)], axis=1)
-        for kd in range(2):
-            grad[:, kd * BLOCK : (kd + 1) * BLOCK] = dot_nn(r, xg[s, y, kd])
+            grad[:, kd * BLOCK : (kd + 1) * BLOCK] = dot_nn(r, rows_of(s, kd, y, range(4)))
 
     def backward(s):
-        for h in range(2):
+        for ps in ((0, 1), (2, 3)):
             for j in (1, 3, 2):
                 b = (y + 4 - j) % 4
-                for q in (2 * h, 2 * h + 1):
-                    for cut in cuts(q):
-                        g_from(s, j, q, *cut).wait_recv()
-                r = jnp.concatenate([resid[s, b, 2 * h], resid[s, b, 2 * h + 1]], axis=1)
+                for p in ps:
+                    g_from(s, j, p).wait_recv()
+                r = jnp.concatenate([resid[s, b, p] for p in ps], axis=1)
                 for kd in range(2):
-                    grad[:, kd * BLOCK : (kd + 1) * BLOCK] += dot_nn(r, xg[s, b, kd, halves[h], :])
+                    grad[:, kd * BLOCK : (kd + 1) * BLOCK] += dot_nn(r, rows_of(s, kd, b, ps))
 
     pieces = [(h, c) for c in range(4) for h in range(2)]
 
@@ -293,10 +307,6 @@
                     wb[part] = new.astype(BF16)
             then(h, c)
 
-    def x_arrived(s, d):
-        for h in range(2):
-            x_sib(s, d, h, incoming=True).wait_recv()
-
     def sent(s):
         for way in range(2):
             for h in range(2):
@@ -305,12 +315,11 @@
         for d in range(4):
             for h in range(2):
                 x_sib(s, d, h).wait_send()
-        for q in range(4):
-            for cut in cuts(q):
-                for j in (1, 2, 3):
-                    y_out(s, j, q, *cut).wait_send()
-                    g_out(s, j, q, *cut).wait_send()
-                z_out(s, q, *cut).wait_send()
+        for p in range(4):
+            for j in (1, 2, 3):
+                y_out(s, j, p).wait_send()
+                g_out(s, j, p).wait_send()
+            z_out(s, p).wait_send()
 
     fast = g < 3
     total_steps = float(3 * STEPS + SLOW_STEPS)
@@ -376,31 +385,43 @@
             late_out(h, c).start()
 
     locals_[1].wait()
-    x_arrived(0, 0)
-    forward_block(0, x)
+    forward(0, 0)
     x_middle(0)
+
+    @pl.when(holds)
+    def _():
+        for b in range(4):
+            stays = jnp.logical_and(b == y, k == y % 2)
+
+            @pl.when(stays)
+            def _():
+                t_local.wait()
+
+            @pl.when(jnp.logical_not(stays))
+            def _():
+                t_from(b).wait_recv()
+
+    gather_y(0, 0)
     x_rest(0)
-    x_arrived(0, 3)
-    forward_block(0, xl)
-    x_arrived(0, 1)
-    forward_block(0, xr_)
+    forward(0, 1)
+    forward(0, 2)
 
     @pl.when(fast)
     def _():
         x_begin(1)
 
+    gather_z(0, 0)
     x_end(0)
-    locals_[6].wait()
-    t_swap(1 - k).wait_recv()
-    x_arrived(0, 2)
-    forward_block(0, xo)
-    gather_y(0)
+    forward(0, 3)
+    for p in (1, 2, 3):
+        gather_y(0, p)
 
     @pl.when(fast)
     def _():
         x_middle(1)
 
-    gather_z(0)
+    for p in (1, 2, 3):
+        gather_z(0, p)
     backward_own(0)
 
     @pl.when(fast)
@@ -422,28 +443,30 @@
         sent(0)
         for i in range(3):
             swap_in(i).wait_send()
-        t_swap(k).wait_send()
+        t_sent()
         for h in range(2):
             slow_out(h).wait_send()
 
     @pl.when(fast)
     def _():
         for s in range(1, STEPS):
+            for p in range(3):
+                forward(s, p)
             x_end(s)
             if s + 1 < STEPS:
                 x_begin(s + 1)
-            for d in (0, 3, 1, 2):
-                x_arrived(s, d)
-            forward_pieces(s)
+            forward(s, 3)
             sent(s - 1)
             if s == 1:
                 for i in range(3):
                     swap_in(i).wait_send()
-                t_swap(k).wait_send()
-            gather_y(s)
+                t_sent()
+            for p in range(4):
+                gather_y(s, p)
             if s + 1 < STEPS:
                 x_middle(s + 1)
-            gather_z(s)
+            for p in range(4):
+                gather_z(s, p)
             backward_own(s)
             if s + 1 < STEPS:
                 x_rest(s + 1)
@@ -552,7 +575,7 @@
             vm((3, 2, 512, PART), F32),
             vm((PART, 1024), F32), vm((PART, 1024), F32), vm((PART, 1024), F32), vm((PART, 1024), F32),
             vm((PART, 1024), BF16),
-            vm((2, n, *tile), BF16),
+            vm((4, n, *tile), BF16),
             vm((4, *tile), F32),
             vm((n, 4, 4, *tile), BF16), vm((n, 4, 4, *tile), BF16),
             vm((4, *tile), F32),
@@ -566,9 +589,9 @@
             vm((2, 4, *tile), F32), vm((4, *tile), F32),
             dma((7,)),
             dma((n, 6)), dma((n, 6)), dma((n, 8)), dma((n, 8)),
-            dma((3,)), dma((3,)), dma, dma,
-            dma((n, 4, 4, max(CUTS))), dma((n, 4, 4, max(CUTS))), dma((n, 4, max(CUTS))), dma((n, 4, max(CUTS))),
-            dma((n, 4, 4, max(CUTS))), dma((n, 4, 4, max(CUTS))),
+            dma((3,)), dma((3,)), dma((2,)), dma((4,)),
+            dma((n, 4, 4)), dma((n, 4, 4)), dma((n, 4)), dma((n, 4)),
+            dma((n, 4, 4)), dma((n, 4, 4)),
             dma((2,)), dma, dma((2,)), dma((2,)), dma((4,)), dma((2,)),
             dma((2, 4)), dma((2, 4)), dma((4, 4)), dma((2, 4)),
             dma((4,)), dma((4,)),

time: 113 us -> 107 us (0.947)
  Pallas kernels: 110 us -> 103 us
    pallas_call x1, Pallas kernels: 110 us -> 103 us  [pseudo_of(): pl.pallas_call(kernel, out_shape=jax.ShapeDtypeStruct((512, 256), F32), i...]
where the time goes in v4:
time: 107 us; the launch traced here: 106 us
  Pallas kernels  103 us (96%)
  other arithmetic  2.29 us (2%)
    pallas_call x1, Pallas kernels, pseudo_of(): pl.pallas_call(kernel, out_shape=jax.ShapeDtypeStruct((512, 256), F32), i...  103 us
    sub x1, other arithmetic, local(): outer_params - outer_rate * (pseudo + momentum_coef * new_moment)  2.29 us

profile of v4, /device:TPU:1, one launch (start us, length us, event | category | flops | bytes accessed | tf_op | source)
XLA Modules:
  0.0 106.5 jit_solution(10974468921240066253)
XLA Ops:
  0.6 0.0 copy-start
  0.6 103.5 %shard_map.77 = f32[512,256]{1,0:T(8,128)} custom-call(f32[512,256]{1,0:T(8,128)} %w_in.1, f32[1,512,256]{2,1,0:T(8,128)} %m_in.1, f32[1,512,256]{2,1,0:T(8,128)} %v_in.1, bf16[1,3,512,512]{3,2,1,0:T(8,128)(2,1)} %x_in.1, bf16[1,3,128,256]{3,2,1,0:T(8,128)(2,1)} %t_in.1), custom_call_target="tpu_custom_call" | custom-call | tf_op jit(solution)/shard_map/pallas_call | solution.py:568
  104.1 0.0 copy-done
  104.2 2.3 %multiply_subtract_fusion = (f32[512,256]{1,0:T(8,128)}, f32[512,256]{1,0:T(8,128)}) fusion(f32[512,256]{1,0:T(8,128)S(1)} %copy-done, f32[512,256]{1,0:T(8,128)} %shard_map.77, f32[512,256]{1,0:T(8,128)} %param.9), kind=kLoop, calls=%fused_computation | loop fusion | flops 786432 | bytes 2621440 | tf_op jit(solution)/shard_map/sub | solution.py:608
Async XLA Ops:
  0.6 103.5 %copy-start = (f32[512,256]{1,0:T(8,128)S(1)}, f32[512,256]{1,0:T(8,128)}, u32[]{:S(2)}) copy-start(f32[512,256]{1,0:T(8,128)} %w_in.1) | copy-start | bytes 1572868

commit v5 on v4

--- a/solution.py
+++ b/solution.py
@@ -597,9 +597,9 @@
             dma((4,)), dma((4,)),
         ],
         compiler_params=pltpu.CompilerParams(
-            collective_id=0, has_side_effects=True, vmem_limit_bytes=63 << 20
+            collective_id=0, has_side_effects=True, vmem_limit_bytes=48 << 20
         ),
-    )(outer_params, first_moment, second_moment, activations, targets)
+    )(*[pltpu.with_memory_space_constraint(a, pltpu.HBM) for a in (outer_params, first_moment, second_moment, activations, targets)])
 
 
 def local(outer_params, first_moment, second_moment, outer_moment, activations, targets):

time: 107 us -> 105 us (0.981)
  other arithmetic: 2.29 us -> 1.09 us
    sub x1, other arithmetic: 2.29 us -> 1.09 us  [local(): outer_params - outer_rate * (pseudo + momentum_coef * new_moment)]
where the time goes in v5:
time: 105 us; the launch traced here: 104 us
  Pallas kernels  103 us (98%)
  other arithmetic  1.09 us (1%)
    pallas_call x1, Pallas kernels, pseudo_of(): pl.pallas_call(kernel, out_shape=jax.ShapeDtypeStruct((512, 256), F32), i...  103 us

profile of v5, /device:TPU:1, one launch (start us, length us, event | category | flops | bytes accessed | tf_op | source)
XLA Modules:
  0.0 104.5 jit_solution(18276138285626135665)
XLA Ops:
  0.6 0.0 copy-start
  0.6 0.0 copy-start.1
  0.7 102.7 %shard_map.77 = f32[512,256]{1,0:T(8,128)S(1)} custom-call(f32[512,256]{1,0:T(8,128)} %w_in.1, f32[1,512,256]{2,1,0:T(8,128)} %m_in.1, f32[1,512,256]{2,1,0:T(8,128)} %v_in.1, bf16[1,3,512,512]{3,2,1,0:T(8,128)(2,1)} %x_in.1, bf16[1,3,128,256]{3,2,1,0:T(8,128)(2,1)} %t_in.1), custom_call_target="tpu_custom_call" | custom-call | tf_op jit(solution)/shard_map/pallas_call | solution.py:568
  103.4 0.0 copy-done
  103.4 0.0 copy-done.1
  103.4 1.1 %multiply_subtract_fusion = (f32[512,256]{1,0:T(8,128)}, f32[512,256]{1,0:T(8,128)}) fusion(f32[512,256]{1,0:T(8,128)S(1)} %copy-done, f32[512,256]{1,0:T(8,128)S(1)} %shard_map.77, f32[512,256]{1,0:T(8,128)S(1)} %copy-done.1), kind=kLoop, calls=%fused_computation | loop fusion | flops 786432 | bytes 2621440 | tf_op jit(solution)/shard_map/sub | solution.py:608
Async XLA Ops:
  0.6 102.7 %copy-start = (f32[512,256]{1,0:T(8,128)S(1)}, f32[512,256]{1,0:T(8,128)}, u32[]{:S(2)}) copy-start(f32[512,256]{1,0:T(8,128)} %w_in.1) | copy-start | bytes 1572868
  0.6 102.7 %copy-start.1 = (f32[512,256]{1,0:T(8,128)S(1)}, f32[512,256]{1,0:T(8,128)}, u32[]{:S(2)}) copy-start(f32[512,256]{1,0:T(8,128)} %param.9) | copy-start | bytes 1572868

commit v6 on v5

--- a/solution.py
+++ b/solution.py
@@ -427,6 +427,7 @@
     @pl.when(fast)
     def _():
         x_rest(1)
+        x_begin(2)
 
     backward(0)
     update(0, nothing)
@@ -453,8 +454,6 @@
             for p in range(3):
                 forward(s, p)
             x_end(s)
-            if s + 1 < STEPS:
-                x_begin(s + 1)
             forward(s, 3)
             sent(s - 1)
             if s == 1:

time: 105 us -> 104 us (level)
  no operation moved by 1% of the time
where the time goes in v6:
time: 104 us; the launch traced here: 103 us
  Pallas kernels  102 us (98%)
  other arithmetic  1.09 us (1%)
    pallas_call x1, Pallas kernels, pseudo_of(): pl.pallas_call(kernel, out_shape=jax.ShapeDtypeStruct((512, 256), F32), i...  102 us

profile of v6, /device:TPU:1, one launch (start us, length us, event | category | flops | bytes accessed | tf_op | source)
XLA Modules:
  0.0 103.5 jit_solution(7142699608884719352)
XLA Ops:
  0.6 0.0 copy-start
  0.6 0.0 copy-start.1
  0.7 101.7 %shard_map.77 = f32[512,256]{1,0:T(8,128)S(1)} custom-call(f32[512,256]{1,0:T(8,128)} %w_in.1, f32[1,512,256]{2,1,0:T(8,128)} %m_in.1, f32[1,512,256]{2,1,0:T(8,128)} %v_in.1, bf16[1,3,512,512]{3,2,1,0:T(8,128)(2,1)} %x_in.1, bf16[1,3,128,256]{3,2,1,0:T(8,128)(2,1)} %t_in.1), custom_call_target="tpu_custom_call" | custom-call | tf_op jit(solution)/shard_map/pallas_call | solution.py:567
  102.4 0.0 copy-done
  102.4 0.0 copy-done.1
  102.4 1.1 %multiply_subtract_fusion = (f32[512,256]{1,0:T(8,128)}, f32[512,256]{1,0:T(8,128)}) fusion(f32[512,256]{1,0:T(8,128)S(1)} %copy-done, f32[512,256]{1,0:T(8,128)S(1)} %shard_map.77, f32[512,256]{1,0:T(8,128)S(1)} %copy-done.1), kind=kLoop, calls=%fused_computation | loop fusion | flops 786432 | bytes 2621440 | tf_op jit(solution)/shard_map/sub | solution.py:607
Async XLA Ops:
  0.6 101.7 %copy-start = (f32[512,256]{1,0:T(8,128)S(1)}, f32[512,256]{1,0:T(8,128)}, u32[]{:S(2)}) copy-start(f32[512,256]{1,0:T(8,128)} %w_in.1) | copy-start | bytes 1572868
  0.6 101.7 %copy-start.1 = (f32[512,256]{1,0:T(8,128)S(1)}, f32[512,256]{1,0:T(8,128)}, u32[]{:S(2)}) copy-start(f32[512,256]{1,0:T(8,128)} %param.9) | copy-start | bytes 1572868
